TPU v7x, 128 devices: a whole 4x4x4 slice. The times are simulated.
128 devices in a mesh: grp: 8 (over x, core), tp: 16 (over z, y).
Axes of the slice: x: 4, y: 4, z: 4, core: 2. Of those that a mesh axis runs over, the one named last changes fastest.
Arguments:
- hidden_states: bfloat16 [2048, 8192], P('grp', 'tp'), may hold values from -6 to 6
- norm_gain: float32 [8192], replicated, may hold values from 0.5 to 1.5
- w_query: bfloat16 [8192, 8192], P(None, 'tp'), may hold values from -0.0625 to 0.0625
- w_key: bfloat16 [8192, 1024], P(None, 'tp'), may hold values from -0.0625 to 0.0625
- w_value: bfloat16 [8192, 1024], P(None, 'tp'), may hold values from -0.0625 to 0.0625
- cache: bfloat16 [16384, 2048], P('grp', 'tp'), may hold values from -82 to 82
- w_out: bfloat16 [8192, 8192], P('tp'), may hold values from -6 to 6
Outputs:
- mixed: bfloat16 [2048, 8192], P('grp', 'tp')
All inputs are finite; a program needn't handle non-finite values.
Results may differ from a plain program's by a relative error of at most 0.03.
Values may be sent and summed in bfloat16 or wider, within the bound.
A program may use at most 128 MiB of HBM per device.

v0:
```python
import math

import jax
import jax.numpy as jnp
from jax import lax
from jax.sharding import Mesh
from jax.sharding import PartitionSpec as P

HEAD_DIM = 128
TP = ("tp_0", "tp_1")


def swapped(array, axis, distance):
    return lax.ppermute(array, axis, [(i, i ^ 1 << distance) for i in range(lax.axis_size(axis))])


def from_everyone(array, axis):
    copies = jnp.broadcast_to(array, (lax.axis_size(axis), *array.shape))
    return lax.all_to_all(copies, axis, split_axis=0, concat_axis=0, tiled=True)


def in_order(pieces, dim):
    pieces = jnp.moveaxis(pieces, 0, dim)
    shape = pieces.shape
    return pieces.reshape(*shape[:dim], shape[dim] * shape[dim + 1], *shape[dim + 2 :])


def gather_directly(array, axis, dim):
    pieces = from_everyone(array, axis)
    return in_order(pieces, dim)


def sent_together(arrays, axis, split_dim, concat_dim, along):
    columns = [a.reshape(*a.shape[:along], -1) for a in arrays]
    both = jnp.concatenate(columns, axis=along)
    whole, at, done = (
        lax.all_to_all(both, axis, split_axis=split_dim, concat_axis=concat_dim, tiled=True),
        0,
        [],
    )
    for a, column in zip(arrays, columns):
        slab = whole[..., at : at + column.shape[along]]
        done.append(slab.reshape(*slab.shape[:along], *a.shape[along:]))
        at += column.shape[along]
    return tuple(done)


def sum_by_axis(terms, axes):
    total = terms.astype(jnp.bfloat16)
    for axis in axes:
        total = lax.psum_scatter(total, axis, scatter_dimension=0, tiled=True)
    return total.astype(jnp.float32)


def rotate(values, positions):
    half = values.shape[-1] // 2
    freqs = 500000.0 ** (-jnp.arange(half, dtype=jnp.float32) * 2.0 / values.shape[-1])
    angles = positions.astype(jnp.float32)[..., None] * freqs
    cosine = jnp.cos(angles)
    sine = jnp.sin(angles)
    first = values[..., :half]
    second = values[..., half:]
    return jnp.concatenate([first * cosine - second * sine, second * cosine + first * sine], -1)


def absorb(state, queries, keys, values, key_start, query_start, heads):
    count = keys.shape[0]
    block = math.gcd(count, 1024)
    steps = count // block
    width = keys.shape[1]
    scale = 1.0 / math.sqrt(width)
    query_pos = query_start + jnp.arange(queries.shape[0], dtype=jnp.int32) // heads

    def visit(carry, item):
        best, total, summed = carry
        key_block, value_block, index = item
        scores = (
            lax.dot_general(
                queries, key_block, (((1,), (1,)), ((), ())), preferred_element_type=jnp.float32
            )
            * scale
        )
        if key_start is not None:
            key_pos = key_start + index * block + jnp.arange(block, dtype=jnp.int32)
            scores = jnp.where(key_pos[None, :] <= query_pos[:, None], scores, -1e30)
        top = jnp.maximum(best, jnp.max(scores, axis=1))
        factor = jnp.exp(best - top)
        weights = jnp.exp(scores - top[:, None])
        total = total * factor + jnp.sum(weights, axis=1)
        summed = summed * factor[:, None] + jnp.dot(
            weights.astype(jnp.bfloat16), value_block, preferred_element_type=jnp.float32
        )
        return ((top, total, summed), None)

    result, unused = lax.scan(
        visit,
        state,
        (
            keys.reshape(steps, block, width),
            values.reshape(steps, block, width),
            jnp.arange(steps, dtype=jnp.int32),
        ),
    )
    return result


def body(hidden_states, norm_gain, w_query, w_key, w_value, cache, w_out):
    rows = hidden_states.shape[0]
    groups = lax.axis_size("grp")
    group = lax.axis_index("grp")
    parity = lax.axis_index(TP) % 2
    whole = lax.all_gather(hidden_states, TP, axis=1, tiled=True).astype(jnp.float32)
    normed = (
        whole * lax.rsqrt(jnp.mean(whole * whole, axis=1, keepdims=True) + 1e-05) * norm_gain
    ).astype(jnp.bfloat16)
    prefix = cache.shape[0] * groups
    first = group * rows
    positions = prefix + first + jnp.arange(rows, dtype=jnp.int32)
    heads = w_query.shape[1] // HEAD_DIM
    lanes = rows * heads
    query = jnp.dot(normed, w_query, preferred_element_type=jnp.float32).reshape(
        rows, heads, HEAD_DIM
    )
    query = rotate(query, positions[:, None]).astype(jnp.bfloat16).reshape(lanes, HEAD_DIM)
    key_part = jnp.dot(normed, w_key, preferred_element_type=jnp.float32)
    value_part = jnp.dot(normed, w_value, preferred_element_type=jnp.float32)
    partner_cache = swapped(cache, TP, 0)
    cache_key = jnp.where(parity == 0, cache, partner_cache)
    cache_value = jnp.where(parity == 0, partner_cache, cache)
    partner_key, partner_value = (
        swapped(key_part.astype(jnp.bfloat16), TP, 0).astype(key_part.dtype),
        swapped(value_part.astype(jnp.bfloat16), TP, 0).astype(value_part.dtype),
    )
    key_full = jnp.where(
        parity == 0,
        jnp.concatenate([key_part, partner_key], 1),
        jnp.concatenate([partner_key, key_part], 1),
    )
    value_full = jnp.where(
        parity == 0,
        jnp.concatenate([value_part, partner_value], 1),
        jnp.concatenate([partner_value, value_part], 1),
    )
    key_new = rotate(key_full, positions).astype(jnp.bfloat16)
    value_new = value_full.astype(jnp.bfloat16)
    start_state = (
        jnp.full((lanes,), -1e30, jnp.float32),
        jnp.zeros((lanes,), jnp.float32),
        jnp.zeros((lanes, HEAD_DIM), jnp.float32),
    )
    every = gather_directly(query, "grp", 0).reshape(groups, lanes, HEAD_DIM)

    def serve(item):
        block_queries, block_index = item
        state = absorb(
            start_state, block_queries, cache_key, cache_value, None, block_index * rows, heads
        )
        return absorb(state, block_queries, key_new, value_new, first, block_index * rows, heads)

    best, total, summed = lax.map(serve, (every, jnp.arange(groups, dtype=jnp.int32)))
    summed, best, total = tuple(
        (
            part.astype(jnp.float32)
            for part in sent_together(
                (
                    summed.astype(jnp.bfloat16),
                    best.astype(jnp.bfloat16),
                    total.astype(jnp.bfloat16),
                ),
                "grp",
                0,
                0,
                2,
            )
        )
    )
    top = jnp.max(best, axis=0)
    factor = jnp.exp(best - top[None, :])
    attended = (
        jnp.sum(summed * factor[:, :, None], axis=0) / jnp.sum(total * factor, axis=0)[:, None]
    )
    attended = attended.astype(jnp.bfloat16).reshape(rows, heads * HEAD_DIM)
    mixed = sum_by_axis(
        lax.dot_general(
            w_out, attended, (((0,), (1,)), ((), ())), preferred_element_type=jnp.float32
        ),
        TP,
    )
    return mixed.T.astype(jnp.bfloat16)


def solution(mesh):
    finer = Mesh(mesh.devices.reshape(mesh.shape["grp"], 4, 4), ("grp", "tp_0", "tp_1"))
    in_specs = (P("grp", TP), P(), P(None, TP), P(None, TP), P(None, TP), P("grp", TP), P(TP, None))
    out_specs = P("grp", TP)
    return jax.shard_map(body, mesh=finer, in_specs=in_specs, out_specs=out_specs, check_vma=False)
```

profile of v0, /device:TPU:0, one launch (start us, length us, event | category | flops | bytes accessed | tf_op | source)
XLA Modules:
  0.0 305.9 jit_solution(13559694169984585403)
XLA Ops:
  7.3 62.4 %all-gather.2.cloned.1.call-done = bf16[256,8192]{1,0:T(8,128)(2,1)} async-done(((bf16[256,512]{1,0:T(8,128)(2,1)}), bf16[256,8192]{1,0:T(8,128)(2,1)}) %all-gather.2.cloned.1.call-update) | async-done | bytes 4194320 | tf_op jit(solution)/shard_map/all_gather | solution.py:112
  69.7 3.3 %fusion.29 = f32[256]{0:T(256)S(1)} fusion(bf16[256,8192]{1,0:T(8,128)(2,1)} %all-gather.2.cloned.1.call-done), kind=kLoop, calls=%fused_computation.46 | loop fusion | flops 6291200 | bytes 4195328 | tf_op jit(solution)/shard_map/reduce_sum | solution.py:114
  73.2 1.5 fusion.49
  74.7 1.3 collective-permute-start.1
  76.5 2.4 fusion.45
  80.3 1.7 broadcast_in_dim.80
  82.0 4.3 %all-to-all-start = ((bf16[8,1024,128]{2,1,0:T(8,128)(2,1)}), bf16[8,1024,128]{2,1,0:T(8,128)(2,1)}, u32[]{:S(2)}, u32[]{:S(2)}) async-start(bf16[8,1024,128]{2,1,0:T(8,128)(2,1)} %broadcast_in_dim.80), calls=%async_computation | async-start | bytes 4194304 | tf_op jit(solution)/shard_map/all_to_all | solution.py:19
  86.4 1.3 collective-permute-start
  87.7 3.9 %fusion.41 = bf16[256,64]{0,1:T(8,128)(2,1)S(1)} fusion(bf16[8192,64]{0,1:T(8,128)(2,1)} %param.15, bf16[256,8192]{1,0:T(8,128)(2,1)} %all-gather.2.cloned.1.call-done, f32[8192]{0:T(1024)S(1)} %copy-done.4, f32[256]{0:T(256)S(1)} %add_rsqrt_fusion), kind=kOutput, calls=%fused_computation.81 | convolution fusion | flops 276824064 | bytes 5309440 | tf_op jit(solution)/shard_map/dot_general | solution.py:126
  91.6 1.1 collective-permute-start.2
  92.7 8.3 %collective-permute-done = bf16[2048,128]{1,0:T(8,128)(2,1)S(1)} collective-permute-done((bf16[2048,128]{1,0:T(8,128)(2,1)S(1)}, bf16[2048,128]{1,0:T(8,128)(2,1)S(1)}, u32[]{:S(2)}, u32[]{:S(2)}) %collective-permute-start) | collective-permute-done | bytes 524320 | tf_op jit(solution)/shard_map/ppermute | solution.py:14
  101.7 11.9 %all-to-all-done = bf16[8,1024,128]{2,1,0:T(8,128)(2,1)} async-done(((bf16[8,1024,128]{2,1,0:T(8,128)(2,1)}), bf16[8,1024,128]{2,1,0:T(8,128)(2,1)}, u32[]{:S(2)}, u32[]{:S(2)}) %all-to-all-start) | async-done | bytes 2097184 | tf_op jit(solution)/shard_map/all_to_all | solution.py:19
  113.6 73.2 %while.47 = (s32[]{:T(128)}, bf16[8,1024]{1,0:T(8,128)(2,1)S(1)}, bf16[8,1024]{1,0:T(8,128)(2,1)S(1)}, bf16[8,1024,128]{1,2,0:T(8,128)(2,1)}, bf16[2048,128]{1,0...) while((s32[]{:T(128)}, bf16[8,1024]{1,0:T(8,128)(2,1)S(1)}, ...), condition=%wide.region_8.9_spmd, body=%wide.region_1.8_spmd.sunk | while | flops 682377472 | bytes 20466068 | solution.py:160
  115.8 5.0 %while.48 = (s32[]{:T(128)}, f32[1024]{0:T(1024)S(1)}, f32[1024]{0:T(1024)S(1)}, f32[1024,128]{1,0:T(8,128)S(1)}, bf16[2,1024,128]{2,1,0:T(8,128)(2,1)S(1)}, /*i...) while((s32[]{:T(128)}, f32[1024]{0:T(1024)S(1)}, ...), condition=%wide.region_5.5_spmd.clone, body=%wide.region_2.4_spmd.clone.sunk | while | flops 545657856 | bytes 14483577 | solution.py:95
  117.3 1.0 fusion.85
  124.9 5.0 %while.48 = (s32[]{:T(128)}, f32[1024]{0:T(1024)S(1)}, f32[1024]{0:T(1024)S(1)}, f32[1024,128]{1,0:T(8,128)S(1)}, bf16[2,1024,128]{2,1,0:T(8,128)(2,1)S(1)}, /*i...) while((s32[]{:T(128)}, f32[1024]{0:T(1024)S(1)}, ...), condition=%wide.region_5.5_spmd.clone, body=%wide.region_2.4_spmd.clone.sunk | while | flops 545657856 | bytes 14483577 | solution.py:95
  126.4 1.0 fusion.85
  134.1 5.0 %while.48 = (s32[]{:T(128)}, f32[1024]{0:T(1024)S(1)}, f32[1024]{0:T(1024)S(1)}, f32[1024,128]{1,0:T(8,128)S(1)}, bf16[2,1024,128]{2,1,0:T(8,128)(2,1)S(1)}, /*i...) while((s32[]{:T(128)}, f32[1024]{0:T(1024)S(1)}, ...), condition=%wide.region_5.5_spmd.clone, body=%wide.region_2.4_spmd.clone.sunk | while | flops 545657856 | bytes 14483577 | solution.py:95
  143.2 5.0 %while.48 = (s32[]{:T(128)}, f32[1024]{0:T(1024)S(1)}, f32[1024]{0:T(1024)S(1)}, f32[1024,128]{1,0:T(8,128)S(1)}, bf16[2,1024,128]{2,1,0:T(8,128)(2,1)S(1)}, /*i...) while((s32[]{:T(128)}, f32[1024]{0:T(1024)S(1)}, ...), condition=%wide.region_5.5_spmd.clone, body=%wide.region_2.4_spmd.clone.sunk | while | flops 545657856 | bytes 14483577 | solution.py:95
  144.7 1.0 fusion.85
  152.4 5.0 %while.48 = (s32[]{:T(128)}, f32[1024]{0:T(1024)S(1)}, f32[1024]{0:T(1024)S(1)}, f32[1024,128]{1,0:T(8,128)S(1)}, bf16[2,1024,128]{2,1,0:T(8,128)(2,1)S(1)}, /*i...) while((s32[]{:T(128)}, f32[1024]{0:T(1024)S(1)}, ...), condition=%wide.region_5.5_spmd.clone, body=%wide.region_2.4_spmd.clone.sunk | while | flops 545657856 | bytes 14483577 | solution.py:95
  153.9 1.0 fusion.85
  156.4 1.0 fusion.85
  161.5 5.0 %while.48 = (s32[]{:T(128)}, f32[1024]{0:T(1024)S(1)}, f32[1024]{0:T(1024)S(1)}, f32[1024,128]{1,0:T(8,128)S(1)}, bf16[2,1024,128]{2,1,0:T(8,128)(2,1)S(1)}, /*i...) while((s32[]{:T(128)}, f32[1024]{0:T(1024)S(1)}, ...), condition=%wide.region_5.5_spmd.clone, body=%wide.region_2.4_spmd.clone.sunk | while | flops 545657856 | bytes 14483577 | solution.py:95
  170.7 5.0 %while.48 = (s32[]{:T(128)}, f32[1024]{0:T(1024)S(1)}, f32[1024]{0:T(1024)S(1)}, f32[1024,128]{1,0:T(8,128)S(1)}, bf16[2,1024,128]{2,1,0:T(8,128)(2,1)S(1)}, /*i...) while((s32[]{:T(128)}, f32[1024]{0:T(1024)S(1)}, ...), condition=%wide.region_5.5_spmd.clone, body=%wide.region_2.4_spmd.clone.sunk | while | flops 545657856 | bytes 14483577 | solution.py:95
  179.8 5.0 %while.48 = (s32[]{:T(128)}, f32[1024]{0:T(1024)S(1)}, f32[1024]{0:T(1024)S(1)}, f32[1024,128]{1,0:T(8,128)S(1)}, bf16[2,1024,128]{2,1,0:T(8,128)(2,1)S(1)}, /*i...) while((s32[]{:T(128)}, f32[1024]{0:T(1024)S(1)}, ...), condition=%wide.region_5.5_spmd.clone, body=%wide.region_2.4_spmd.clone.sunk | while | flops 545657856 | bytes 14483577 | solution.py:95
  183.8 1.0 fusion.85
  186.8 1.9 pad_maximum_fusion
  188.7 31.3 %all_to_all.10 = bf16[8,1024,130]{1,2,0:T(8,128)(2,1)S(1)} all-to-all(bf16[8,1024,130]{1,2,0:T(8,128)(2,1)S(1)} %pad_maximum_fusion), channel_id=1, replica_groups=mesh['grp'=8,'tp_0'=4,'tp_1'=4] {'grp'}, dimensions={0} | all-to-all | bytes 4259840 | tf_op jit(solution)/shard_map/all_to_all | solution.py:37
  221.4 7.7 %fusion.28 = bf16[8192,256]{0,1:T(8,128)(2,1)} fusion(bf16[512,8192]{1,0:T(8,128)(2,1)} %param.17, f32[256,512]{1,0:T(8,128)S(1)} %reduce_sum.54, f32[32,8,4,128]{3,2,1,0:T(4,128)S(1)} %bitcast.92), kind=kOutput, calls=%fused_computation.45 | convolution fusion | flops 2149842944 | bytes 13631488 | tf_op jit(solution)/shard_map/dot_general | solution.py:184
  229.2 44.6 %reduce-scatter.3.cloned.1.call-done = bf16[2048,256]{0,1:T(8,128)(2,1)} async-done(((bf16[8192,256]{0,1:T(8,128)(2,1)}), bf16[2048,256]{0,1:T(8,128)(2,1)}) %reduce-scatter.3.cloned.1.call-update) | async-done | bytes 1048592 | tf_op jit(solution)/shard_map/reduce_scatter | solution.py:51
  273.8 25.7 %reduce-scatter.5.cloned.1.call-done = bf16[512,256]{0,1:T(8,128)(2,1)} async-done(((bf16[2048,256]{0,1:T(8,128)(2,1)}), bf16[512,256]{0,1:T(8,128)(2,1)}) %reduce-scatter.5.cloned.1.call-update) | async-done | bytes 262160 | tf_op jit(solution)/shard_map/reduce_scatter | solution.py:51
  (267 shorter events, 66.1 us)
Async XLA Ops:
  6.5 66.4 %copy-start = (bf16[8192,64]{0,1:T(8,128)(2,1)S(1)}, bf16[8192,64]{0,1:T(8,128)(2,1)}, u32[]{:S(2)}) copy-start(bf16[8192,64]{0,1:T(8,128)(2,1)} %param.14) | copy-start | bytes 3145732
  6.5 66.4 %copy-start.4 = (f32[8192]{0:T(1024)S(1)}, f32[8192]{0:T(1024)}, u32[]{:S(2)}) copy-start(f32[8192]{0:T(1024)} %param.12) | copy-start | bytes 98308
  6.5 63.2 %all-gather.2.cloned.1.call-start = ((), (), s32[]{:S(2)}) async-start(), calls=%async_computation.4 | async-start | bytes 4456448 | tf_op jit(solution)/shard_map/all_gather | solution.py:112
  69.7 3.4 %copy-start.1 = (bf16[256,8192]{1,0:T(8,128)(2,1)S(1)}, bf16[256,8192]{1,0:T(8,128)(2,1)}, u32[]{:S(2)}) copy-start(bf16[256,8192]{1,0:T(8,128)(2,1)} %all-gather.2.cloned.1.call-done) | copy-start | bytes 12582916
  73.1 3.4 %copy-start.3 = (bf16[8192,512]{1,0:T(8,128)(2,1)S(1)}, bf16[8192,512]{1,0:T(8,128)(2,1)}, u32[]{:S(2)}) copy-start(bf16[8192,512]{1,0:T(8,128)(2,1)} %param.13) | copy-start | bytes 25165828
  74.7 4.4 %collective-permute-start.1 = (bf16[256,64]{0,1:T(8,128)(2,1)S(1)}, bf16[256,64]{0,1:T(8,128)(2,1)S(1)}, u32[]{:S(2)}, u32[]{:S(2)}) collective-permute-start(bf16[256,64]{0,1:T(8,128)(2,1)S(1)} %get-tuple-element.383), channel_id=1, source_target_pairs={{0,1},{1,0},{2,3},{3,2},{4,5},{5,4},{6,7},{7,6},{8,9},{9,8},{10,11... | collective-permute-start | bytes 98312 | tf_op jit(solution)/shard_map/ppermute | solution.py:14
  79.7 6.7 %copy-start.2 = (bf16[2048,128]{1,0:T(8,128)(2,1)S(1)}, bf16[2048,128]{1,0:T(8,128)(2,1)}, u32[]{:S(2)}) copy-start(bf16[2048,128]{1,0:T(8,128)(2,1)} %param.16) | copy-start | bytes 1572868
  82.0 31.6 %all-to-all-start = ((bf16[8,1024,128]{2,1,0:T(8,128)(2,1)}), bf16[8,1024,128]{2,1,0:T(8,128)(2,1)}, u32[]{:S(2)}, u32[]{:S(2)}) async-start(bf16[8,1024,128]{2,1,0:T(8,128)(2,1)} %broadcast_in_dim.80), calls=%async_computation | async-start | bytes 4194304 | tf_op jit(solution)/shard_map/all_to_all | solution.py:19
  86.4 187.4 %reduce-scatter.3.cloned.1.call-start = ((), (), s32[]{:S(2)}) async-start(), calls=%async_computation.5 | async-start | bytes 5242880 | tf_op jit(solution)/shard_map/reduce_scatter | solution.py:51
  86.4 14.6 %collective-permute-start = (bf16[2048,128]{1,0:T(8,128)(2,1)S(1)}, bf16[2048,128]{1,0:T(8,128)(2,1)S(1)}, u32[]{:S(2)}, u32[]{:S(2)}) collective-permute-start(bf16[2048,128]{1,0:T(8,128)(2,1)S(1)} %copy-done.2), channel_id=1, source_target_pairs={{0,1},{1,0},{2,3},{3,2},{4,5},{5,4},{6,7},{7,6},{8,9},{9,8},{10,11... | collective-permute-start | bytes 1572872 | tf_op jit(solution)/shard_map/ppermute | solution.py:14
  91.6 9.8 %collective-permute-start.2 = (bf16[256,64]{0,1:T(8,128)(2,1)S(1)}, bf16[256,64]{0,1:T(8,128)(2,1)S(1)}, u32[]{:S(2)}, u32[]{:S(2)}) collective-permute-start(bf16[256,64]{0,1:T(8,128)(2,1)S(1)} %fusion.41), channel_id=1, source_target_pairs={{0,1},{1,0},{2,3},{3,2},{4,5},{5,4},{6,7},{7,6},{8,9},{9,8},{10,11... | collective-permute-start | bytes 98312 | tf_op jit(solution)/shard_map/ppermute | solution.py:14
  229.1 70.3 %reduce-scatter.5.cloned.1.call-start = ((), (), s32[]{:S(2)}) async-start(), calls=%async_computation.6 | async-start | bytes 1310720 | tf_op jit(solution)/shard_map/reduce_scatter | solution.py:51
Sparse Core Ops, SparseCore 0:
  9.5 60.1 all-gather.1
  229.2 44.4 reduce-scatter.2
  276.3 23.0 reduce-scatter.4
where the time goes:
time: 307 us; the launch traced here: 306 us
  waiting for transfers between devices  154 us (50%)
  matrix products  48.3 us (16%)
  blocking collectives  31.3 us (10%)
  local copies, waits for them, and re-layouts  24.4 us (8%)
  other arithmetic  20.5 us (7%)
  between operations  13.4 us (4%)
  starting transfers between devices  8.07 us (3%)
  loops' own time  6.1 us (2%)
    reduce_scatter x2, waiting for transfers between devices, sum_by_axis(): total = lax.psum_scatter(total, axis, scatter_dimension=0, tiled=True)  70.2 us
    all_gather x1, waiting for transfers between devices, body(): lax.all_gather(hidden_states, TP, axis=1, tiled=True).astype(jnp.float32)  62.4 us
    all_to_all x1, blocking collectives, sent_together(): lax.all_to_all(both, axis, split_axis=split_dim, concat_axis=concat_dim,...  31.3 us
    dot_general x24, matrix products, visit(): jnp.dot(weights.astype(jnp.bfloat16), value_block, preferred_element_type...  18.8 us
    dot_general x24, matrix products, visit(): lax.dot_general(queries, key_block, (((1,), (1,)), ((), ())), preferred_e...  14 us
    reduce_sum x24, other arithmetic, visit(): total = total * factor + jnp.sum(weights, axis=1)  13.1 us
    all_to_all x1, waiting for transfers between devices, from_everyone(): return lax.all_to_all(copies, axis, split_axis=0, concat_axis=0, tiled=True)  11.9 us
    ppermute x3, waiting for transfers between devices, swapped(): lax.ppermute(array, axis, [(i, i ^ 1 << distance) for i in range(lax.axis...  8.59 us
  transfers between devices with their start and end apart: 7, of which 6 were waited for; matrix products, arithmetic and copies ran while one was open for 2% of the time, Pallas kernels for 0%

commit v1 on v0

v1 whole, which is shorter than its diff:
```python
import functools
import math

import jax
import jax.numpy as jnp
from jax import lax
from jax.experimental import pallas as pl
from jax.experimental.pallas import tpu as pltpu
from jax.sharding import PartitionSpec as P

HEAD_DIM = 128
MESH = pl.DeviceIdType.MESH
BF = jnp.bfloat16
F32 = jnp.float32
ROWS = 256
FEATURES = 8192
CHUNK = 256
NEG = -1e30
VMEM = pltpu.MemorySpace.VMEM


def place():
    grp = lax.axis_index("grp")
    tp = lax.axis_index("tp")
    return grp // 2, grp % 2, tp // 4, tp % 4


def wrap(i):
    return lax.rem(i + 8, 4)


def greet(partners):
    barrier = pltpu.get_barrier_semaphore()
    for partner in partners:
        pl.semaphore_signal(barrier, inc=1, device_id=partner, device_id_type=MESH)
    pl.semaphore_wait(barrier, len(partners))


def remote(src, dst, send, recv, partner):
    return pltpu.make_async_remote_copy(
        src_ref=src, dst_ref=dst, send_sem=send, recv_sem=recv, device_id=partner, device_id_type=MESH
    )


def project_kernel(
    hid, gain, cos, sin, wq_hbm, wk_hbm, wv_hbm, cache,
    q_out, kv_out,
    got, wq, wk, wv, acc, squares, part, partner_part, fresh,
    send, recv, load, swap_send, swap_recv,
):
    x, core, z, y = place()
    grp = 2 * x + core
    parity = lax.rem(y, 2)

    def at(dz, dy):
        return wrap(z + dz) * 4 + wrap(y + dy)

    def to(dz, dy):
        return {"grp": grp, "tp": at(dz, dy)}

    def chunk(half, a, b):
        return 2 * (at(b, a) if half == 0 else at(a, b)) + half

    def first(half, d):
        return to(0, d) if half == 0 else to(d, 0)

    def second(half, d):
        return to(d, 0) if half == 0 else to(0, d)

    partner = {"grp": grp, "tp": z * 4 + y + 1 - 2 * parity}
    sibling = {"grp": grp + 1 - 2 * core, "tp": z * 4 + y}
    loads = [
        pltpu.make_async_copy(wq_hbm, wq, load.at[0]),
        pltpu.make_async_copy(wk_hbm, wk, load.at[1]),
        pltpu.make_async_copy(wv_hbm, wv, load.at[2]),
    ]
    for one in loads:
        one.start()
    own_cache = pltpu.make_async_copy(cache, kv_out.at[parity, core, pl.ds(0, 2048)], load.at[3])
    own_cache.start()
    for half in range(2):
        got[chunk(half, 0, 0)] = hid[:, half * CHUNK : (half + 1) * CHUNK]
    greet([to(0, 1), to(0, -1), to(1, 0), to(-1, 0), sibling])

    TOP, BOTTOM, ALL = pl.ds(0, 128), pl.ds(128, 128), pl.ds(0, 256)

    def message(half, m, idx, rows, partner):
        ref = got.at[idx, rows]
        return remote(ref, ref, send.at[half, m], recv.at[half, m], partner)

    for m, d in ((0, 1), (1, -1)):
        for half in range(2):
            message(half, m, chunk(half, 0, 0), ALL, first(half, d)).start()
    for m, d in ((4, 1), (5, -1)):
        for half in range(2):
            message(half, m, chunk(half, 0, 0), ALL, second(half, d)).start()
    mine = kv_out.at[parity, core, pl.ds(0, 2048)]
    swaps = [
        remote(cache, mine, swap_send.at[0], swap_recv.at[0], partner),
        remote(cache, mine, swap_send.at[1], swap_recv.at[1], sibling),
    ]
    for one in swaps:
        one.start()

    acc[...] = jnp.zeros_like(acc)
    squares[...] = jnp.zeros_like(squares)

    def absorb(idx):
        h = got[idx].astype(F32)
        sq = h * h
        squares[...] += sq[:, :128] + sq[:, 128:]
        scaled = (h * gain[pl.ds(idx, 1), :]).astype(BF)
        depth = pl.ds(pl.multiple_of(idx * CHUNK, CHUNK), CHUNK)
        acc[:, :512] += jnp.dot(scaled, wq[depth, :], preferred_element_type=F32)
        wkv = jnp.concatenate([wk[depth, :], wv[depth, :]], axis=1)
        acc[:, 512:] += jnp.dot(scaled, wkv, preferred_element_type=F32)

    def absorb_all(count, index_of):
        def step(i, carry):
            absorb(index_of(i))
            return carry

        lax.fori_loop(0, count, step, 0)

    def pick(flag, a, b):
        return jnp.where(flag == 0, a, b)

    def chunk_of(half, a, b):
        return pick(half, chunk(0, a, b), chunk(1, a, b))

    def arrived(half, m, idx, rows):
        message(half, m, idx, rows, sibling).wait_recv()

    def spread(half, j, idx):
        message(half, 4 + 4 * j, idx, ALL, second(half, 1)).start()
        message(half, 5 + 4 * j, idx, ALL, second(half, -1)).start()

    for one in loads:
        one.wait()
    absorb_all(2, lambda i: chunk_of(i, 0, 0))
    for half in range(2):
        idx = chunk(half, -1, 0)
        arrived(half, 0, idx, ALL)
        message(half, 2, idx, TOP, first(half, 1)).start()
        spread(half, 1, idx)
    for half in range(2):
        idx = chunk(half, 1, 0)
        arrived(half, 1, idx, ALL)
        message(half, 3, idx, BOTTOM, first(half, -1)).start()
        spread(half, 2, idx)
    absorb_all(4, lambda i: chunk_of(i % 2, 2 * (i // 2) - 1, 0))

    def neighbours(j, a):
        for half in range(2):
            idx = chunk(half, a, -1)
            arrived(half, 4 + 4 * j, idx, ALL)
            message(half, 6 + 4 * j, idx, TOP, second(half, 1)).start()
            idx = chunk(half, a, 1)
            arrived(half, 5 + 4 * j, idx, ALL)
            message(half, 7 + 4 * j, idx, BOTTOM, second(half, -1)).start()
        absorb_all(4, lambda i: chunk_of(i % 2, a, 2 * (i // 2) - 1))

    def opposite(j, a):
        for half in range(2):
            idx = chunk(half, a, 2)
            arrived(half, 6 + 4 * j, idx, TOP)
            arrived(half, 7 + 4 * j, idx, BOTTOM)
        absorb_all(2, lambda i: chunk_of(i, a, 2))

    neighbours(0, 0)
    for half in range(2):
        idx = chunk(half, 2, 0)
        arrived(half, 2, idx, TOP)
        arrived(half, 3, idx, BOTTOM)
        spread(half, 3, idx)
    absorb_all(2, lambda i: chunk_of(i, 2, 0))

    def sweep(j, carry):
        neighbours(j, jnp.where(j == 1, -1, j - 1))
        return carry

    lax.fori_loop(1, 4, sweep, 0)
    theirs = kv_out.at[1 - parity, core, pl.ds(0, 2048)]
    remote(cache, theirs, swap_send.at[0], swap_recv.at[0], partner).wait_recv()
    passed = remote(theirs, theirs, swap_send.at[2], swap_recv.at[2], sibling)
    passed.start()

    def sweep_far(j, carry):
        opposite(j, jnp.where(j == 0, 0, jnp.where(j == 1, -1, j - 1)))
        return carry

    lax.fori_loop(0, 4, sweep_far, 0)

    mean = jnp.sum(squares[...], axis=1, keepdims=True) * (1.0 / FEATURES)
    root = lax.rsqrt(mean + 1e-05)
    lane = lax.broadcasted_iota(jnp.int32, (ROWS, 128), 1)
    own = acc[:, 512:] * root
    part[...] = own.astype(BF)
    swap = remote(part, partner_part, swap_send.at[3], swap_recv.at[3], partner)
    swap.start()
    c, s = cos[...], sin[...]

    def rope(v):
        return v * c + pltpu.roll(v, 64, 1) * s

    scale = math.log2(math.e) / math.sqrt(HEAD_DIM)
    parts = q_out.shape[0]
    tokens = ROWS // parts
    for head in range(4):
        turned = (rope(acc[:, head * 128 : (head + 1) * 128] * root) * scale).astype(BF)
        for i in range(parts):
            q_out[i, head * tokens : (head + 1) * tokens, :] = turned[i * tokens : (i + 1) * tokens, :]
    swap.wait()
    other = partner_part[...].astype(F32)
    left = jnp.where(parity == 0, own, other)
    right = jnp.where(parity == 0, other, own)
    key = jnp.where(lane < 64, left, pltpu.roll(right, 64, 1))
    value = jnp.where(lane < 64, pltpu.roll(left, 64, 1), right)
    fresh[0] = rope(key).astype(BF)
    fresh[1] = value.astype(BF)
    spot = kv_out.at[:, core, pl.ds(2048, 256)]
    keep = pltpu.make_async_copy(fresh, spot, load.at[0])
    keep.start()
    give = remote(fresh, spot, swap_send.at[4], swap_recv.at[4], sibling)
    give.start()
    keep.wait()
    give.wait_send()
    remote(fresh, kv_out.at[:, 1 - core, pl.ds(2048, 256)], swap_send.at[4], swap_recv.at[4], sibling).wait_recv()
    own_cache.wait()
    swaps[0].wait_send()
    swaps[1].wait_send()
    remote(cache, kv_out.at[parity, 1 - core, pl.ds(0, 2048)], swap_send.at[1], swap_recv.at[1], sibling).wait_recv()
    passed.wait_send()
    remote(
        cache, kv_out.at[1 - parity, 1 - core, pl.ds(0, 2048)], swap_send.at[2], swap_recv.at[2], sibling
    ).wait_recv()

    def drain(half, m, rows):
        message(half, m, chunk(half, 0, 0), rows, sibling).wait_send()

    for half in range(2):
        drain(half, 0, ALL)
        drain(half, 1, ALL)
        drain(half, 2, TOP)
        drain(half, 3, BOTTOM)
        for j in range(4):
            drain(half, 4 + 4 * j, ALL)
            drain(half, 5 + 4 * j, ALL)
            drain(half, 6 + 4 * j, TOP)
            drain(half, 7 + 4 * j, BOTTOM)


def project(hid, gain, cos, sin, wq, wk, wv, cache, parts):
    whole = pl.BlockSpec(memory_space=VMEM)
    left = pl.BlockSpec(memory_space=pl.ANY)
    dma = pltpu.SemaphoreType.DMA
    return pl.pallas_call(
        project_kernel,
        out_shape=(
            jax.ShapeDtypeStruct((parts, 1024 // parts, 128), BF),
            jax.ShapeDtypeStruct((2, 2, 2304, 128), BF),
        ),
        in_specs=[whole] * 4 + [left] * 4,
        out_specs=(whole, left),
        scratch_shapes=[
            pltpu.VMEM((32, ROWS, CHUNK), BF),
            pltpu.VMEM((FEATURES, 512), BF),
            pltpu.VMEM((FEATURES, 64), BF),
            pltpu.VMEM((FEATURES, 64), BF),
            pltpu.VMEM((ROWS, 640), F32),
            pltpu.VMEM((ROWS, 128), F32),
            pltpu.VMEM((ROWS, 128), BF),
            pltpu.VMEM((ROWS, 128), BF),
            pltpu.VMEM((2, ROWS, 128), BF),
            dma((2, 20)),
            dma((2, 20)),
            dma((4,)),
            dma((5,)),
            dma((5,)),
        ],
        compiler_params=pltpu.CompilerParams(
            collective_id=0, has_side_effects=True, vmem_limit_bytes=60 << 20
        ),
        name="project",
    )(hid, gain, cos, sin, wq, wk, wv, cache)


PIECES = ((0, 1024), (1024, 1024), (2048, 256))


def attend_kernel(
    q, kv, att,
    qs, ob, oin, stat, stat_in, sa, sb, top_a, top_b, summed, total,
    q_send, q_recv, o_send, o_recv, t_send, t_recv,
):
    x, core, z, y = place()
    tp = z * 4 + y
    parts, rows, width = q.shape
    tokens = rows // 4

    def chip(i):
        return {"grp": 2 * wrap(i) + core, "tp": tp}

    greet([chip(x + 1), chip(x + 2), chip(x + 3)])
    order = (1, 3, 2)

    def query(c, d):
        return remote(q.at[c], qs.at[d, c], q_send.at[d, c], q_recv.at[d, c], chip(x + d))

    for c in range(parts):
        for d in order:
            query(c, d).start()
    qs[0] = q[...]
    diff = lax.broadcasted_iota(jnp.int32, (rows, 256), 1) - lax.rem(
        lax.broadcasted_iota(jnp.int32, (rows, 256), 0), tokens
    )

    def block_of(i):
        c, k = i // 4, lax.rem(i, 4)
        k = jnp.where(c == 0, k, lax.rem(k + 1, 4))
        return c, jnp.where(k == 2, 3, jnp.where(k == 3, 2, k))

    def prepare(i):
        c, slot = block_of(i)

        @pl.when(slot != 0)
        def _():
            remote(q.at[0], qs.at[slot, c], q_send.at[slot, c], q_recv.at[slot, c], chip(x + 1)).wait_recv()

    def score(i, n, s_ref, top_ref):
        c, slot = block_of(i)
        b, (start, size) = n // 3, PIECES[n % 3]
        s = lax.dot_general(
            qs[slot, c], kv[0, b, start : start + size, :], (((1,), (1,)), ((), ())), preferred_element_type=F32
        )
        if size == 256:
            ahead = (2 * wrap(x - slot) + core - 2 * x - b) * ROWS + c * tokens
            s = jnp.where(diff <= ahead, s, NEG)
        s_ref[:, b * 2304 + start : b * 2304 + start + size] = s
        top = s[:, :128]
        for k in range(1, size // 128):
            top = jnp.maximum(top, s[:, k * 128 : (k + 1) * 128])
        top_ref[...] = top if n == 0 else jnp.maximum(top_ref[...], top)

    def weigh(n, s_ref, best):
        b, (start, size) = n // 3, PIECES[n % 3]
        s = s_ref[:, b * 2304 + start : b * 2304 + start + size]
        w = jnp.exp2(s - best)
        t = w[:, :128]
        for k in range(1, size // 128):
            t = t + w[:, k * 128 : (k + 1) * 128]
        o = jnp.dot(w.astype(BF), kv[1, b, start : start + size, :], preferred_element_type=F32)
        if n == 0:
            total[...] = t
            summed[...] = o
        else:
            total[...] += t
            summed[...] += o

    lane = lax.broadcasted_iota(jnp.int32, (rows, 128), 1)

    def settle(i, best):
        c, slot = block_of(i)
        ob[slot, c] = summed[...].astype(BF)
        t = jnp.sum(total[...], axis=1, keepdims=True)
        both = jnp.where(lane == 0, best, t)
        stat[slot, c] = both.T[:8, :]

        @pl.when(slot != 0)
        def _():
            home = chip(x - slot)
            remote(ob.at[slot, c], oin.at[slot, c], o_send.at[slot, c], o_recv.at[slot, c], home).start()
            remote(stat.at[slot, c], stat_in.at[slot, c], t_send.at[slot, c], t_recv.at[slot, c], home).start()

    def finish(c):
        for d in order:
            remote(ob.at[d, c], oin.at[d, c], o_send.at[d, c], o_recv.at[d, c], chip(x + 1)).wait_recv()
            remote(stat.at[d, c], stat_in.at[d, c], t_send.at[d, c], t_recv.at[d, c], chip(x + 1)).wait_recv()
        stats = [stat[0, c], stat_in[1, c], stat_in[2, c], stat_in[3, c]]
        tops = [s[0:1, :] for s in stats]
        peak = jnp.maximum(jnp.maximum(tops[0], tops[1]), jnp.maximum(tops[2], tops[3]))
        factors = [jnp.exp2(t - peak) for t in tops]
        whole = sum(f * s[1:2, :] for f, s in zip(factors, stats))
        inverse = 1.0 / whole
        row = lax.broadcasted_iota(jnp.int32, (128, rows), 0)
        table = jnp.zeros((128, rows), F32)
        for d in range(4):
            table = jnp.where(row == d, factors[d] * inverse, table)
        columns = table.T
        out = ob[0, c].astype(F32) * columns[:, 0:1]
        for d in range(1, 4):
            out = out + oin[d, c].astype(F32) * columns[:, d : d + 1]
        out = out.astype(BF)
        place_ = pl.ds(pl.multiple_of(c * tokens, tokens), tokens)
        for head in range(4):
            att[place_, head * 128 : (head + 1) * 128] = out[head * tokens : (head + 1) * tokens, :]

    blocks = 4 * parts
    prepare(0)
    for n in range(6):
        score(0, n, sa, top_a)

    def half_step(i, now, top_now, later, top_later):
        nxt = jnp.minimum(i + 1, blocks - 1)

        @pl.when(i + 1 < blocks)
        def _():
            prepare(nxt)

        best = jnp.max(top_now[...], axis=1, keepdims=True)
        for n in range(6):
            score(nxt, n, later, top_later)
            weigh(n, now, best)
        settle(i, best)

    def step(p, carry):
        half_step(2 * p, sa, top_a, sb, top_b)
        half_step(2 * p + 1, sb, top_b, sa, top_a)
        return carry

    lax.fori_loop(0, blocks // 2, step, 0)
    for c in range(parts):
        finish(c)
    for c in range(parts):
        for d in order:
            query(c, d).wait_send()
            remote(ob.at[d, c], oin.at[d, c], o_send.at[d, c], o_recv.at[d, c], chip(x + 1)).wait_send()
            remote(stat.at[d, c], stat_in.at[d, c], t_send.at[d, c], t_recv.at[d, c], chip(x + 1)).wait_send()


def attend(q, kv):
    parts, rows, width = q.shape
    whole = pl.BlockSpec(memory_space=VMEM)
    dma = pltpu.SemaphoreType.DMA
    return pl.pallas_call(
        attend_kernel,
        out_shape=jax.ShapeDtypeStruct((ROWS, 512), BF),
        in_specs=[whole] * 2,
        out_specs=whole,
        scratch_shapes=[
            pltpu.VMEM((4, parts, rows, 128), BF),
            pltpu.VMEM((4, parts, rows, 128), BF),
            pltpu.VMEM((4, parts, rows, 128), BF),
            pltpu.VMEM((4, parts, 8, rows), F32),
            pltpu.VMEM((4, parts, 8, rows), F32),
            pltpu.VMEM((rows, 4608), F32),
            pltpu.VMEM((rows, 4608), F32),
            pltpu.VMEM((rows, 128), F32),
            pltpu.VMEM((rows, 128), F32),
            pltpu.VMEM((rows, 128), F32),
            pltpu.VMEM((rows, 128), F32),
        ]
        + [dma((4, parts))] * 6,
        compiler_params=pltpu.CompilerParams(
            collective_id=1, has_side_effects=True, vmem_limit_bytes=60 << 20
        ),
        name="attend",
    )(q, kv)


def mix_kernel(att, w_hbm, out, w, terms, relay, inbox, terms2, relay2, inbox2, send, recv, load):
    x, core, z, y = place()
    grp = 2 * x + core
    rows = att.shape[0]
    half_rows = rows // 2

    def to(dz, dy):
        return {"grp": grp, "tp": wrap(z + dz) * 4 + wrap(y + dy)}

    def first(half, d):
        return to(0, d) if half == 0 else to(d, 0)

    def second(half, d):
        return to(d, 0) if half == 0 else to(0, d)

    here = ((y, z), (z, y))
    fetch = pltpu.make_async_copy(w_hbm, w, load.at[0])
    fetch.start()
    greet([to(0, 1), to(0, -1), to(1, 0), to(-1, 0)])
    fetch.wait()
    a_val = att[...]

    def fill(half, d):
        a = wrap(here[half][0] + d)

        def step(b, carry):
            t = b * 4 + a if half == 0 else a * 4 + b
            start = pl.multiple_of(t * 512 + half * 256, 256)
            r = jnp.dot(a_val, w[:, pl.ds(start, 256)], preferred_element_type=F32).astype(BF)
            terms[half, a, 0, b] = r[:half_rows]
            terms[half, a, 1, b] = r[half_rows:]
            return carry

        lax.fori_loop(0, 4, step, 0)

    def copy(half, m, src, dst, partner):
        return remote(src, dst, send.at[half, m], recv.at[half, m], partner)

    started = []

    def launch(*args):
        one = copy(*args)
        one.start()
        started.append(one)

    def add(dst, src):
        dst[...] = (dst[...].astype(F32) + src[...].astype(F32)).astype(BF)

    def block(half, d, ch):
        return terms.at[half, wrap(here[half][0] + d), ch]

    def block2(half, d, ch):
        return terms2.at[half, ch, wrap(here[half][1] + d)]

    for half in range(2):
        fill(half, 2)
        launch(half, 0, block(half, 2, 0), relay.at[half, 0], first(half, 1))
        launch(half, 1, block(half, 2, 1), relay.at[half, 1], first(half, -1))
    for half in range(2):
        fill(half, 1)
        launch(half, 2, block(half, 1, 1), inbox.at[half, 0, 1], first(half, 1))
        fill(half, -1)
        launch(half, 4, block(half, -1, 0), inbox.at[half, 1, 0], first(half, -1))
    for half in range(2):
        copy(half, 0, relay.at[half, 0], relay.at[half, 0], first(half, 1)).wait_recv()
        add(block(half, 1, 0), relay.at[half, 0])
        launch(half, 3, block(half, 1, 0), inbox.at[half, 0, 0], first(half, 1))
        copy(half, 1, relay.at[half, 1], relay.at[half, 1], first(half, 1)).wait_recv()
        add(block(half, -1, 1), relay.at[half, 1])
        launch(half, 5, block(half, -1, 1), inbox.at[half, 1, 1], first(half, -1))
    for half in range(2):
        fill(half, 0)
    for half in range(2):
        for m, side, ch in ((2, 0, 1), (4, 1, 0), (3, 0, 0), (5, 1, 1)):
            ref = inbox.at[half, side, ch]
            copy(half, m, ref, ref, first(half, 1)).wait_recv()

        def merge(b, carry):
            for ch in range(2):
                got = terms[half, here[half][0], ch, b].astype(F32)
                got = got + inbox[half, 0, ch, b].astype(F32) + inbox[half, 1, ch, b].astype(F32)
                terms2[half, ch, b] = got.astype(BF)
            return carry

        lax.fori_loop(0, 4, merge, 0)
        launch(half, 6, block2(half, 2, 0), relay2.at[half, 0], second(half, 1))
        launch(half, 7, block2(half, 2, 1), relay2.at[half, 1], second(half, -1))
        launch(half, 8, block2(half, 1, 1), inbox2.at[half, 0, 1], second(half, 1))
        launch(half, 10, block2(half, -1, 0), inbox2.at[half, 1, 0], second(half, -1))
    for half in range(2):
        copy(half, 6, relay2.at[half, 0], relay2.at[half, 0], first(half, 1)).wait_recv()
        add(block2(half, 1, 0), relay2.at[half, 0])
        launch(half, 9, block2(half, 1, 0), inbox2.at[half, 0, 0], second(half, 1))
        copy(half, 7, relay2.at[half, 1], relay2.at[half, 1], first(half, 1)).wait_recv()
        add(block2(half, -1, 1), relay2.at[half, 1])
        launch(half, 11, block2(half, -1, 1), inbox2.at[half, 1, 1], second(half, -1))
    for half in range(2):
        for m, side, ch in ((8, 0, 1), (10, 1, 0), (9, 0, 0), (11, 1, 1)):
            ref = inbox2.at[half, side, ch]
            copy(half, m, ref, ref, first(half, 1)).wait_recv()
        for ch in range(2):
            got = terms2[half, ch, here[half][1]].astype(F32)
            got = got + inbox2[half, 0, ch].astype(F32) + inbox2[half, 1, ch].astype(F32)
            out[ch * half_rows : (ch + 1) * half_rows, half * 256 : (half + 1) * 256] = got.astype(BF)
    for one in started:
        one.wait_send()


def mix(att, w_out):
    whole = pl.BlockSpec(memory_space=VMEM)
    dma = pltpu.SemaphoreType.DMA
    h = ROWS // 2
    return pl.pallas_call(
        mix_kernel,
        out_shape=jax.ShapeDtypeStruct((ROWS, 512), BF),
        in_specs=[whole, pl.BlockSpec(memory_space=pl.ANY)],
        out_specs=whole,
        scratch_shapes=[
            pltpu.VMEM((512, FEATURES), BF),
            pltpu.VMEM((2, 4, 2, 4, h, 256), BF),
            pltpu.VMEM((2, 2, 4, h, 256), BF),
            pltpu.VMEM((2, 2, 2, 4, h, 256), BF),
            pltpu.VMEM((2, 2, 4, h, 256), BF),
            pltpu.VMEM((2, 2, h, 256), BF),
            pltpu.VMEM((2, 2, 2, h, 256), BF),
            dma((2, 12)),
            dma((2, 12)),
            dma((1,)),
        ],
        compiler_params=pltpu.CompilerParams(
            collective_id=2, has_side_effects=True, vmem_limit_bytes=60 << 20
        ),
        name="mix",
    )(att, w_out)


def turns(first):
    half = HEAD_DIM // 2
    freqs = 500000.0 ** (-jnp.arange(half, dtype=F32) * 2.0 / HEAD_DIM)
    angles = (first + jnp.arange(ROWS, dtype=jnp.int32)).astype(F32)[:, None] * freqs
    cosine, sine = jnp.cos(angles), jnp.sin(angles)
    return jnp.concatenate([cosine, cosine], 1), jnp.concatenate([-sine, sine], 1)


def body(prefix, parts, hidden_states, norm_gain, w_query, w_key, w_value, cache, w_out):
    cos, sin = turns(prefix + lax.axis_index("grp") * ROWS)
    gain = norm_gain.reshape(FEATURES // CHUNK, CHUNK)
    q, kv = project(hidden_states, gain, cos, sin, w_query, w_key, w_value, cache, parts)
    return mix(attend(q, kv), w_out)


def solution(mesh):
    in_specs = (P("grp", "tp"), P(), P(None, "tp"), P(None, "tp"), P(None, "tp"), P("grp", "tp"), P("tp", None))
    return jax.shard_map(
        functools.partial(body, 16384, 2),
        mesh=mesh,
        in_specs=in_specs,
        out_specs=P("grp", "tp"),
        check_vma=False,
    )
```

time: 307 us -> 134 us (0.44)
  waiting for transfers between devices: 154 us -> 0 us
  Pallas kernels: 0 us -> 125 us
  matrix products: 48.3 us -> 0 us
  blocking collectives: 31.3 us -> 0 us
  other arithmetic: 20.5 us -> 1.39 us
  local copies, waits for them, and re-layouts: 24.4 us -> 7.66 us
  between operations: 13.4 us -> 0.04 us
  starting transfers between devices: 8.07 us -> 0 us
  loops' own time: 6.1 us -> 0 us
    pallas_call x0 -> x3, Pallas kernels: none -> 125 us  [the longest x1 47.4 us: project(): pl.pallas_call(project_kernel, out_shape=(jax.ShapeDtypeStruct((parts, 10...]
    reduce_scatter x2 -> x0, waiting for transfers between devices: 70.2 us -> none  [sum_by_axis(): total = lax.psum_scatter(total, axis, scatter_dimension=0, tiled=True)]
    all_gather x1 -> x0, waiting for transfers between devices: 62.4 us -> none  [body(): lax.all_gather(hidden_states, TP, axis=1, tiled=True).astype(jnp.float32)]
    dot_general x52 -> x0, matrix products: 48.3 us -> none  [the longest x24 18.8 us: visit(): jnp.dot(weights.astype(jnp.bfloat16), value_block, preferred_element_type...]
    all_to_all x1 -> x0, blocking collectives: 31.3 us -> none  [sent_together(): lax.all_to_all(both, axis, split_axis=split_dim, concat_axis=concat_dim,...]
    reduce_sum x27 -> x0, other arithmetic: 16.8 us -> none  [the longest x24 13.1 us: visit(): total = total * factor + jnp.sum(weights, axis=1)]
    all_to_all x1 -> x0, waiting for transfers between devices: 11.9 us -> none  [from_everyone(): return lax.all_to_all(copies, axis, split_axis=0, concat_axis=0, tiled=True)]
    ppermute x3 -> x0, waiting for transfers between devices: 8.59 us -> none  [swapped(): lax.ppermute(array, axis, [(i, i ^ 1 << distance) for i in range(lax.axis...]
  transfers between devices with their start and end apart: 7 -> 0, of which waited for: 6 -> 0; matrix products, arithmetic and copies ran while one was open for 2% -> 0% of each run, Pallas kernels for 0% -> 0%
where the time goes in v1:
time: 134 us
  Pallas kernels  125 us (93%)
  local copies, waits for them, and re-layouts  7.66 us (6%)
  other arithmetic  1.39 us (1%)
    pallas_call x1, Pallas kernels, project(): pl.pallas_call(project_kernel, out_shape=(jax.ShapeDtypeStruct((parts, 10...  47.4 us
    pallas_call x1, Pallas kernels, attend(): pl.pallas_call(attend_kernel, out_shape=jax.ShapeDtypeStruct((ROWS, 512),...  45.2 us
    pallas_call x1, Pallas kernels, mix(): pl.pallas_call(mix_kernel, out_shape=jax.ShapeDtypeStruct((ROWS, 512), BF...  32.3 us
    unnamed x5, local copies, waits for them, and re-layouts  6.2 us

profile of v1, /device:TPU:0, one launch (start us, length us, event | category | flops | bytes accessed | tf_op | source)
XLA Modules:
  0.0 134.0 jit_solution(11912141840445405349)
XLA Ops:
  0.0 0.0 copy-start
  0.0 1.5 %reshape.14.gain = f32[32,256]{1,0:T(8,128)} reshape(f32[8192]{0:T(1024)} %param.8) | data formatting | bytes 65536 | tf_op jit(solution)/shard_map/reshape | solution.py:607
  1.5 0.5 fusion
  2.0 0.8 pad_maximum_fusion
  2.9 2.7 %copy.8.wk_hbm = bf16[8192,64]{1,0:T(8,128)(2,1)} copy(bf16[8192,64]{0,1:T(8,128)(2,1)} %param.10) | data formatting | bytes 2097152 | tf_op args[3]
  5.6 0.0 copy-done
  5.6 1.8 %copy.9.wv_hbm = bf16[8192,64]{1,0:T(8,128)(2,1)} copy(bf16[8192,64]{0,1:T(8,128)(2,1)S(1)} %copy-done) | data formatting | bytes 2097152 | tf_op args[4]
  7.4 47.4 %project.1 = (bf16[2,512,128]{2,1,0:T(8,128)(2,1)}, bf16[2,2,2304,128]{3,2,1,0:T(8,128)(2,1)}) custom-call(bf16[256,512]{1,0:T(8,128)(2,1)} %hid.1, f32[32,256]{1,0:T(8,128)} %reshape.14.gain, f32[256,128]{1,0:T(8,128)} %get-tuple-element.12.cos, f32[256,128]{1,0:T(8,128)} %get-tuple-element.13.sin, bf16[8192,512]{1,0:T(8,128)(2,1)} %wq_hbm.1, ...), custom_call_target="tpu_custom_call" | custom-call | tf_op jit(solution)/shard_map/project/pallas_call | solution.py:257
  54.8 45.2 %attend.1.att = bf16[256,512]{1,0:T(8,128)(2,1)} custom-call(bf16[2,512,128]{2,1,0:T(8,128)(2,1)} %get-tuple-element.7.q, bf16[2,2,2304,128]{3,2,1,0:T(8,128)(2,1)} %get-tuple-element.8.kv), custom_call_target="tpu_custom_call" | custom-call | tf_op jit(solution)/shard_map/attend/pallas_call | solution.py:435
  100.0 32.3 %mix.1 = bf16[256,512]{1,0:T(8,128)(2,1)} custom-call(bf16[256,512]{1,0:T(8,128)(2,1)} %attend.1.att, bf16[512,8192]{1,0:T(8,128)(2,1)} %w_hbm.1), custom_call_target="tpu_custom_call" | custom-call | tf_op jit(solution)/shard_map/mix/pallas_call | solution.py:573
  132.4 1.7 %copy.11 = bf16[256,512]{1,0:T(8,128)(2,1)} copy(bf16[256,512]{1,0:T(8,128)(2,1)} %mix.1) | data formatting | bytes 524288
  (2 shorter events, 0.0 us)
Async XLA Ops:
  0.0 5.6 %copy-start = (bf16[8192,64]{0,1:T(8,128)(2,1)S(1)}, bf16[8192,64]{0,1:T(8,128)(2,1)}, u32[]{:S(2)}) copy-start(bf16[8192,64]{0,1:T(8,128)(2,1)} %param.11) | copy-start | bytes 3145732

commit v2 on v1

--- a/solution.py
+++ b/solution.py
@@ -3,6 +3,7 @@
 
 import jax
 import jax.numpy as jnp
+import numpy as np
 from jax import lax
 from jax.experimental import pallas as pl
 from jax.experimental.pallas import tpu as pltpu
@@ -43,9 +44,9 @@
 
 
 def project_kernel(
-    hid, gain, cos, sin, wq_hbm, wk_hbm, wv_hbm, cache,
+    prefix, hid, gain, freqs, wq_hbm, wk_hbm, wv_hbm, cache,
     q_out, kv_out,
-    got, wq, wk, wv, acc, squares, part, partner_part, fresh,
+    got, wq, wkv, acc, squares, cos, sin, part, partner_part, fresh,
     send, recv, load, swap_send, swap_recv,
 ):
     x, core, z, y = place()
@@ -71,8 +72,8 @@
     sibling = {"grp": grp + 1 - 2 * core, "tp": z * 4 + y}
     loads = [
         pltpu.make_async_copy(wq_hbm, wq, load.at[0]),
-        pltpu.make_async_copy(wk_hbm, wk, load.at[1]),
-        pltpu.make_async_copy(wv_hbm, wv, load.at[2]),
+        pltpu.make_async_copy(wk_hbm, wkv.at[pl.ds(0, 64)], load.at[1]),
+        pltpu.make_async_copy(wv_hbm, wkv.at[pl.ds(64, 64)], load.at[2]),
     ]
     for one in loads:
         one.start()
@@ -109,11 +110,12 @@
         h = got[idx].astype(F32)
         sq = h * h
         squares[...] += sq[:, :128] + sq[:, 128:]
-        scaled = (h * gain[pl.ds(idx, 1), :]).astype(BF)
         depth = pl.ds(pl.multiple_of(idx * CHUNK, CHUNK), CHUNK)
+        scaled = (h * gain[:, depth]).astype(BF)
         acc[:, :512] += jnp.dot(scaled, wq[depth, :], preferred_element_type=F32)
-        wkv = jnp.concatenate([wk[depth, :], wv[depth, :]], axis=1)
-        acc[:, 512:] += jnp.dot(scaled, wkv, preferred_element_type=F32)
+        acc[:, 512:] += lax.dot_general(
+            scaled, wkv[:, depth], (((1,), (1,)), ((), ())), preferred_element_type=F32
+        )
 
     def absorb_all(count, index_of):
         def step(i, carry):
@@ -135,6 +137,12 @@
         message(half, 4 + 4 * j, idx, ALL, second(half, 1)).start()
         message(half, 5 + 4 * j, idx, ALL, second(half, -1)).start()
 
+    lane = lax.broadcasted_iota(jnp.int32, (ROWS, 128), 1)
+    row = lax.broadcasted_iota(jnp.int32, (ROWS, 128), 0)
+    angles = (row + (prefix + grp * ROWS)).astype(F32) * freqs[...]
+    cos[...] = jnp.cos(angles)
+    sine = jnp.sin(angles)
+    sin[...] = jnp.where(lane < 64, -sine, sine)
     for one in loads:
         one.wait()
     absorb_all(2, lambda i: chunk_of(i, 0, 0))
@@ -193,7 +201,6 @@
 
     mean = jnp.sum(squares[...], axis=1, keepdims=True) * (1.0 / FEATURES)
     root = lax.rsqrt(mean + 1e-05)
-    lane = lax.broadcasted_iota(jnp.int32, (ROWS, 128), 1)
     own = acc[:, 512:] * root
     part[...] = own.astype(BF)
     swap = remote(part, partner_part, swap_send.at[3], swap_recv.at[3], partner)
@@ -250,24 +257,27 @@
             drain(half, 7 + 4 * j, BOTTOM)
 
 
-def project(hid, gain, cos, sin, wq, wk, wv, cache, parts):
+def project(hid, gain, wq, wk, wv, cache, prefix, parts):
     whole = pl.BlockSpec(memory_space=VMEM)
     left = pl.BlockSpec(memory_space=pl.ANY)
     dma = pltpu.SemaphoreType.DMA
+    half = np.arange(HEAD_DIM // 2, dtype=np.float64) * 2.0 / HEAD_DIM
+    freqs = jnp.asarray(np.tile(500000.0**-half, 2)[None, :], F32)
     return pl.pallas_call(
-        project_kernel,
+        functools.partial(project_kernel, prefix),
         out_shape=(
             jax.ShapeDtypeStruct((parts, 1024 // parts, 128), BF),
             jax.ShapeDtypeStruct((2, 2, 2304, 128), BF),
         ),
-        in_specs=[whole] * 4 + [left] * 4,
+        in_specs=[whole] * 3 + [left] * 4,
         out_specs=(whole, left),
         scratch_shapes=[
             pltpu.VMEM((32, ROWS, CHUNK), BF),
             pltpu.VMEM((FEATURES, 512), BF),
-            pltpu.VMEM((FEATURES, 64), BF),
-            pltpu.VMEM((FEATURES, 64), BF),
+            pltpu.VMEM((128, FEATURES), BF),
             pltpu.VMEM((ROWS, 640), F32),
+            pltpu.VMEM((ROWS, 128), F32),
+            pltpu.VMEM((ROWS, 128), F32),
             pltpu.VMEM((ROWS, 128), F32),
             pltpu.VMEM((ROWS, 128), BF),
             pltpu.VMEM((ROWS, 128), BF),
@@ -282,26 +292,41 @@
             collective_id=0, has_side_effects=True, vmem_limit_bytes=60 << 20
         ),
         name="project",
-    )(hid, gain, cos, sin, wq, wk, wv, cache)
+    )(hid, gain, freqs, wq, wk.T, wv.T, cache)
 
 
 PIECES = ((0, 1024), (1024, 1024), (2048, 256))
 
 
-def attend_kernel(
-    q, kv, att,
-    qs, ob, oin, stat, stat_in, sa, sb, top_a, top_b, summed, total,
-    q_send, q_recv, o_send, o_recv, t_send, t_recv,
+def attend_mix_kernel(
+    q, kv, w_hbm, out,
+    w, vx, qs, ob, oin, stat, stat_in, sa, sb, top_a, top_b, summed, att,
+    terms, relay, inbox, terms2, relay2, inbox2,
+    q_send, q_recv, o_send, o_recv, t_send, t_recv, send, recv, load,
 ):
     x, core, z, y = place()
+    grp = 2 * x + core
     tp = z * 4 + y
     parts, rows, width = q.shape
     tokens = rows // 4
+    half_rows = tokens // 2
 
     def chip(i):
         return {"grp": 2 * wrap(i) + core, "tp": tp}
 
-    greet([chip(x + 1), chip(x + 2), chip(x + 3)])
+    def to(dz, dy):
+        return {"grp": grp, "tp": wrap(z + dz) * 4 + wrap(y + dy)}
+
+    def first(half, d):
+        return to(0, d) if half == 0 else to(d, 0)
+
+    def second(half, d):
+        return to(d, 0) if half == 0 else to(0, d)
+
+    here = ((y, z), (z, y))
+    fetch = pltpu.make_async_copy(w_hbm, w, load.at[0])
+    fetch.start()
+    greet([chip(x + 1), chip(x + 2), chip(x + 3), to(0, 1), to(0, -1), to(1, 0), to(-1, 0)])
     order = (1, 3, 2)
 
     def query(c, d):
@@ -311,6 +336,9 @@
         for d in order:
             query(c, d).start()
     qs[0] = q[...]
+    for b in range(2):
+        vx[b, :, :128] = kv[1, b]
+        vx[b, :, 128:] = jnp.ones((2304, 128), BF)
     diff = lax.broadcasted_iota(jnp.int32, (rows, 256), 1) - lax.rem(
         lax.broadcasted_iota(jnp.int32, (rows, 256), 0), tokens
     )
@@ -344,26 +372,16 @@
 
     def weigh(n, s_ref, best):
         b, (start, size) = n // 3, PIECES[n % 3]
-        s = s_ref[:, b * 2304 + start : b * 2304 + start + size]
-        w = jnp.exp2(s - best)
-        t = w[:, :128]
-        for k in range(1, size // 128):
-            t = t + w[:, k * 128 : (k + 1) * 128]
-        o = jnp.dot(w.astype(BF), kv[1, b, start : start + size, :], preferred_element_type=F32)
-        if n == 0:
-            total[...] = t
-            summed[...] = o
-        else:
-            total[...] += t
-            summed[...] += o
+        w_ = jnp.exp2(s_ref[:, b * 2304 + start : b * 2304 + start + size] - best)
+        o = jnp.dot(w_.astype(BF), vx[b, start : start + size, :], preferred_element_type=F32)
+        summed[...] = o if n == 0 else summed[...] + o
 
     lane = lax.broadcasted_iota(jnp.int32, (rows, 128), 1)
 
     def settle(i, best):
         c, slot = block_of(i)
-        ob[slot, c] = summed[...].astype(BF)
-        t = jnp.sum(total[...], axis=1, keepdims=True)
-        both = jnp.where(lane == 0, best, t)
+        ob[slot, c] = summed[:, :128].astype(BF)
+        both = jnp.where(lane == 0, best, summed[:, 128:])
         stat[slot, c] = both.T[:8, :]
 
         @pl.when(slot != 0)
@@ -387,13 +405,114 @@
         for d in range(4):
             table = jnp.where(row == d, factors[d] * inverse, table)
         columns = table.T
-        out = ob[0, c].astype(F32) * columns[:, 0:1]
+        o = ob[0, c].astype(F32) * columns[:, 0:1]
         for d in range(1, 4):
-            out = out + oin[d, c].astype(F32) * columns[:, d : d + 1]
-        out = out.astype(BF)
-        place_ = pl.ds(pl.multiple_of(c * tokens, tokens), tokens)
+            o = o + oin[d, c].astype(F32) * columns[:, d : d + 1]
+        o = o.astype(BF)
         for head in range(4):
-            att[place_, head * 128 : (head + 1) * 128] = out[head * tokens : (head + 1) * tokens, :]
+            att[:, head * 128 : (head + 1) * 128] = o[head * tokens : (head + 1) * tokens, :]
+
+    def fill(c, half, d):
+        a = wrap(here[half][0] + d)
+
+        def step(b, carry):
+            t = b * 4 + a if half == 0 else a * 4 + b
+            start = pl.multiple_of(t * 512 + half * 256, 256)
+            r = jnp.dot(att[...], w[:, pl.ds(start, 256)], preferred_element_type=F32).astype(BF)
+            terms[c, half, a, 0, b] = r[:half_rows]
+            terms[c, half, a, 1, b] = r[half_rows:]
+            return carry
+
+        lax.fori_loop(0, 4, step, 0)
+
+    def copy(c, half, m, src, dst, partner):
+        return remote(src, dst, send.at[c, half, m], recv.at[c, half, m], partner)
+
+    def moves(c, half):
+        def block(d, ch):
+            return terms.at[c, half, wrap(here[half][0] + d), ch]
+
+        def block2(d, ch):
+            return terms2.at[c, half, ch, wrap(here[half][1] + d)]
+
+        ends = (
+            (block(2, 0), relay.at[c, half, 0], first(half, 1)),
+            (block(2, 1), relay.at[c, half, 1], first(half, -1)),
+            (block(1, 1), inbox.at[c, half, 0, 1], first(half, 1)),
+            (block(1, 0), inbox.at[c, half, 0, 0], first(half, 1)),
+            (block(-1, 0), inbox.at[c, half, 1, 0], first(half, -1)),
+            (block(-1, 1), inbox.at[c, half, 1, 1], first(half, -1)),
+            (block2(2, 0), relay2.at[c, half, 0], second(half, 1)),
+            (block2(2, 1), relay2.at[c, half, 1], second(half, -1)),
+            (block2(1, 1), inbox2.at[c, half, 0, 1], second(half, 1)),
+            (block2(1, 0), inbox2.at[c, half, 0, 0], second(half, 1)),
+            (block2(-1, 0), inbox2.at[c, half, 1, 0], second(half, -1)),
+            (block2(-1, 1), inbox2.at[c, half, 1, 1], second(half, -1)),
+        )
+        return (lambda m: copy(c, half, m, *ends[m])), ends
+
+    def add(dst, src):
+        dst[...] = (dst[...].astype(F32) + src[...].astype(F32)).astype(BF)
+
+    def stage0(c):
+        finish(c)
+        for half in range(2):
+            sends, _ = moves(c, half)
+            fill(c, half, 2)
+            sends(0).start()
+            sends(1).start()
+        for half in range(2):
+            sends, _ = moves(c, half)
+            fill(c, half, 1)
+            sends(2).start()
+            fill(c, half, -1)
+            sends(4).start()
+        for half in range(2):
+            fill(c, half, 0)
+
+    def stage1(c):
+        for half in range(2):
+            sends, ends = moves(c, half)
+            for m, k in ((0, 3), (1, 5)):
+                sends(m).wait_recv()
+                add(ends[k][0], ends[m][1])
+                sends(k).start()
+
+    def stage2(c):
+        for half in range(2):
+            sends, _ = moves(c, half)
+            for m in (2, 4, 3, 5):
+                sends(m).wait_recv()
+
+            def merge(b, carry):
+                for ch in range(2):
+                    got = terms[c, half, here[half][0], ch, b].astype(F32)
+                    got = got + inbox[c, half, 0, ch, b].astype(F32) + inbox[c, half, 1, ch, b].astype(F32)
+                    terms2[c, half, ch, b] = got.astype(BF)
+                return carry
+
+            lax.fori_loop(0, 4, merge, 0)
+            for m in (6, 7, 8, 10):
+                sends(m).start()
+
+    def stage3(c):
+        for half in range(2):
+            sends, ends = moves(c, half)
+            for m, k in ((6, 9), (7, 11)):
+                sends(m).wait_recv()
+                add(ends[k][0], ends[m][1])
+                sends(k).start()
+
+    def stage4(c):
+        for half in range(2):
+            sends, _ = moves(c, half)
+            for m in (8, 10, 9, 11):
+                sends(m).wait_recv()
+            for ch in range(2):
+                got = terms2[c, half, ch, here[half][1]].astype(F32)
+                got = got + inbox2[c, half, 0, ch].astype(F32) + inbox2[c, half, 1, ch].astype(F32)
+                start = c * tokens + ch * half_rows
+                out[start : start + half_rows, half * 256 : (half + 1) * 256] = got.astype(BF)
 
     blocks = 4 * parts
     prepare(0)
@@ -414,30 +533,56 @@
         settle(i, best)
 
     def step(p, carry):
+        @pl.when(p == 3)
+        def _():
+            stage1(0)
+
         half_step(2 * p, sa, top_a, sb, top_b)
+
+        @pl.when(p == 2)
+        def _():
+            fetch.wait()
+            stage0(0)
+
+        @pl.when(p == 3)
+        def _():
+            stage2(0)
+
         half_step(2 * p + 1, sb, top_b, sa, top_a)
         return carry
 
     lax.fori_loop(0, blocks // 2, step, 0)
-    for c in range(parts):
-        finish(c)
+    stage3(0)
+    stage0(1)
+    stage4(0)
+    stage1(1)
+    stage2(1)
+    stage3(1)
+    stage4(1)
     for c in range(parts):
         for d in order:
             query(c, d).wait_send()
             remote(ob.at[d, c], oin.at[d, c], o_send.at[d, c], o_recv.at[d, c], chip(x + 1)).wait_send()
             remote(stat.at[d, c], stat_in.at[d, c], t_send.at[d, c], t_recv.at[d, c], chip(x + 1)).wait_send()
-
-
-def attend(q, kv):
+        for half in range(2):
+            sends, _ = moves(c, half)
+            for m in range(12):
+                sends(m).wait_send()
+
+
+def attend_mix(q, kv, w_out):
     parts, rows, width = q.shape
     whole = pl.BlockSpec(memory_space=VMEM)
     dma = pltpu.SemaphoreType.DMA
+    h = rows // 8
     return pl.pallas_call(
-        attend_kernel,
+        attend_mix_kernel,
         out_shape=jax.ShapeDtypeStruct((ROWS, 512), BF),
-        in_specs=[whole] * 2,
+        in_specs=[whole, whole, pl.BlockSpec(memory_space=pl.ANY)],
         out_specs=whole,
         scratch_shapes=[
+            pltpu.VMEM((512, FEATURES), BF),
+            pltpu.VMEM((2, 2304, 256), BF),
             pltpu.VMEM((4, parts, rows, 128), BF),
             pltpu.VMEM((4, parts, rows, 128), BF),
             pltpu.VMEM((4, parts, rows, 128), BF),
@@ -447,166 +592,28 @@
             pltpu.VMEM((rows, 4608), F32),
             pltpu.VMEM((rows, 128), F32),
             pltpu.VMEM((rows, 128), F32),
-            pltpu.VMEM((rows, 128), F32),
-            pltpu.VMEM((rows, 128), F32),
+            pltpu.VMEM((rows, 256), F32),
+            pltpu.VMEM((rows // 4, 512), BF),
+            pltpu.VMEM((parts, 2, 4, 2, 4, h, 256), BF),
+            pltpu.VMEM((parts, 2, 2, 4, h, 256), BF),
+            pltpu.VMEM((parts, 2, 2, 2, 4, h, 256), BF),
+            pltpu.VMEM((parts, 2, 2, 4, h, 256), BF),
+            pltpu.VMEM((parts, 2, 2, h, 256), BF),
+            pltpu.VMEM((parts, 2, 2, 2, h, 256), BF),
         ]
-        + [dma((4, parts))] * 6,
+        + [dma((4, parts))] * 6
+        + [dma((parts, 2, 12)), dma((parts, 2, 12)), dma((1,))],
         compiler_params=pltpu.CompilerParams(
             collective_id=1, has_side_effects=True, vmem_limit_bytes=60 << 20
         ),
-        name="attend",
-    )(q, kv)
-
-
-def mix_kernel(att, w_hbm, out, w, terms, relay, inbox, terms2, relay2, inbox2, send, recv, load):
-    x, core, z, y = place()
-    grp = 2 * x + core
-    rows = att.shape[0]
-    half_rows = rows // 2
-
-    def to(dz, dy):
-        return {"grp": grp, "tp": wrap(z + dz) * 4 + wrap(y + dy)}
-
-    def first(half, d):
-        return to(0, d) if half == 0 else to(d, 0)
-
-    def second(half, d):
-        return to(d, 0) if half == 0 else to(0, d)
-
-    here = ((y, z), (z, y))
-    fetch = pltpu.make_async_copy(w_hbm, w, load.at[0])
-    fetch.start()
-    greet([to(0, 1), to(0, -1), to(1, 0), to(-1, 0)])
-    fetch.wait()
-    a_val = att[...]
-
-    def fill(half, d):
-        a = wrap(here[half][0] + d)
-
-        def step(b, carry):
-            t = b * 4 + a if half == 0 else a * 4 + b
-            start = pl.multiple_of(t * 512 + half * 256, 256)
-            r = jnp.dot(a_val, w[:, pl.ds(start, 256)], preferred_element_type=F32).astype(BF)
-            terms[half, a, 0, b] = r[:half_rows]
-            terms[half, a, 1, b] = r[half_rows:]
-            return carry
-
-        lax.fori_loop(0, 4, step, 0)
-
-    def copy(half, m, src, dst, partner):
-        return remote(src, dst, send.at[half, m], recv.at[half, m], partner)
-
-    started = []
-
-    def launch(*args):
-        one = copy(*args)
-        one.start()
-        started.append(one)
-
-    def add(dst, src):
-        dst[...] = (dst[...].astype(F32) + src[...].astype(F32)).astype(BF)
-
-    def block(half, d, ch):
-        return terms.at[half, wrap(here[half][0] + d), ch]
-
-    def block2(half, d, ch):
-        return terms2.at[half, ch, wrap(here[half][1] + d)]
-
-    for half in range(2):
-        fill(half, 2)
-        launch(half, 0, block(half, 2, 0), relay.at[half, 0], first(half, 1))
-        launch(half, 1, block(half, 2, 1), relay.at[half, 1], first(half, -1))
-    for half in range(2):
-        fill(half, 1)
-        launch(half, 2, block(half, 1, 1), inbox.at[half, 0, 1], first(half, 1))
-        fill(half, -1)
-        launch(half, 4, block(half, -1, 0), inbox.at[half, 1, 0], first(half, -1))
-    for half in range(2):
-        copy(half, 0, relay.at[half, 0], relay.at[half, 0], first(half, 1)).wait_recv()
-        add(block(half, 1, 0), relay.at[half, 0])
-        launch(half, 3, block(half, 1, 0), inbox.at[half, 0, 0], first(half, 1))
-        copy(half, 1, relay.at[half, 1], relay.at[half, 1], first(half, 1)).wait_recv()
-        add(block(half, -1, 1), relay.at[half, 1])
-        launch(half, 5, block(half, -1, 1), inbox.at[half, 1, 1], first(half, -1))
-    for half in range(2):
-        fill(half, 0)
-    for half in range(2):
-        for m, side, ch in ((2, 0, 1), (4, 1, 0), (3, 0, 0), (5, 1, 1)):
-            ref = inbox.at[half, side, ch]
-            copy(half, m, ref, ref, first(half, 1)).wait_recv()
-
-        def merge(b, carry):
-            for ch in range(2):
-                got = terms[half, here[half][0], ch, b].astype(F32)
-                got = got + inbox[half, 0, ch, b].astype(F32) + inbox[half, 1, ch, b].astype(F32)
-                terms2[half, ch, b] = got.astype(BF)
-            return carry
-
-        lax.fori_loop(0, 4, merge, 0)
-        launch(half, 6, block2(half, 2, 0), relay2.at[half, 0], second(half, 1))
-        launch(half, 7, block2(half, 2, 1), relay2.at[half, 1], second(half, -1))
-        launch(half, 8, block2(half, 1, 1), inbox2.at[half, 0, 1], second(half, 1))
-        launch(half, 10, block2(half, -1, 0), inbox2.at[half, 1, 0], second(half, -1))
-    for half in range(2):
-        copy(half, 6, relay2.at[half, 0], relay2.at[half, 0], first(half, 1)).wait_recv()
-        add(block2(half, 1, 0), relay2.at[half, 0])
-        launch(half, 9, block2(half, 1, 0), inbox2.at[half, 0, 0], second(half, 1))
-        copy(half, 7, relay2.at[half, 1], relay2.at[half, 1], first(half, 1)).wait_recv()
-        add(block2(half, -1, 1), relay2.at[half, 1])
-        launch(half, 11, block2(half, -1, 1), inbox2.at[half, 1, 1], second(half, -1))
-    for half in range(2):
-        for m, side, ch in ((8, 0, 1), (10, 1, 0), (9, 0, 0), (11, 1, 1)):
-            ref = inbox2.at[half, side, ch]
-            copy(half, m, ref, ref, first(half, 1)).wait_recv()
-        for ch in range(2):
-            got = terms2[half, ch, here[half][1]].astype(F32)
-            got = got + inbox2[half, 0, ch].astype(F32) + inbox2[half, 1, ch].astype(F32)
-            out[ch * half_rows : (ch + 1) * half_rows, half * 256 : (half + 1) * 256] = got.astype(BF)
-    for one in started:
-        one.wait_send()
-
-
-def mix(att, w_out):
-    whole = pl.BlockSpec(memory_space=VMEM)
-    dma = pltpu.SemaphoreType.DMA
-    h = ROWS // 2
-    return pl.pallas_call(
-        mix_kernel,
-        out_shape=jax.ShapeDtypeStruct((ROWS, 512), BF),
-        in_specs=[whole, pl.BlockSpec(memory_space=pl.ANY)],
-        out_specs=whole,
-        scratch_shapes=[
-            pltpu.VMEM((512, FEATURES), BF),
-            pltpu.VMEM((2, 4, 2, 4, h, 256), BF),
-            pltpu.VMEM((2, 2, 4, h, 256), BF),
-            pltpu.VMEM((2, 2, 2, 4, h, 256), BF),
-            pltpu.VMEM((2, 2, 4, h, 256), BF),
-            pltpu.VMEM((2, 2, h, 256), BF),
-            pltpu.VMEM((2, 2, 2, h, 256), BF),
-            dma((2, 12)),
-            dma((2, 12)),
-            dma((1,)),
-        ],
-        compiler_params=pltpu.CompilerParams(
-            collective_id=2, has_side_effects=True, vmem_limit_bytes=60 << 20
-        ),
-        name="mix",
-    )(att, w_out)
-
-
-def turns(first):
-    half = HEAD_DIM // 2
-    freqs = 500000.0 ** (-jnp.arange(half, dtype=F32) * 2.0 / HEAD_DIM)
-    angles = (first + jnp.arange(ROWS, dtype=jnp.int32)).astype(F32)[:, None] * freqs
-    cosine, sine = jnp.cos(angles), jnp.sin(angles)
-    return jnp.concatenate([cosine, cosine], 1), jnp.concatenate([-sine, sine], 1)
+        name="attend_mix",
+    )(q, kv, w_out)
 
 
 def body(prefix, parts, hidden_states, norm_gain, w_query, w_key, w_value, cache, w_out):
-    cos, sin = turns(prefix + lax.axis_index("grp") * ROWS)
-    gain = norm_gain.reshape(FEATURES // CHUNK, CHUNK)
-    q, kv = project(hidden_states, gain, cos, sin, w_query, w_key, w_value, cache, parts)
-    return mix(attend(q, kv), w_out)
+    gain = norm_gain.reshape(1, FEATURES)
+    q, kv = project(hidden_states, gain, w_query, w_key, w_value, cache, prefix, parts)
+    return attend_mix(q, kv, w_out)
 
 
 def solution(mesh):

time: 134 us -> 117 us (0.87)
  Pallas kernels: 125 us -> 115 us
  local copies, waits for them, and re-layouts: 7.66 us -> 1.67 us
  other arithmetic: 1.39 us -> 0 us
    pallas_call x3 -> x2, Pallas kernels: 125 us -> 115 us  [the longest x1 67.5 us: attend_mix(): pl.pallas_call(attend_mix_kernel, out_shape=jax.ShapeDtypeStruct((ROWS, 5...]
    unnamed x5 -> x1, local copies, waits for them, and re-layouts: 6.2 us -> 1.67 us
    reshape x1 -> x0, local copies, waits for them, and re-layouts: 1.45 us -> none  [body(): gain = norm_gain.reshape(FEATURES // CHUNK, CHUNK)]
where the time goes in v2:
time: 117 us
  Pallas kernels  115 us (98%)
  local copies, waits for them, and re-layouts  1.67 us (1%)
    pallas_call x1, Pallas kernels, attend_mix(): pl.pallas_call(attend_mix_kernel, out_shape=jax.ShapeDtypeStruct((ROWS, 5...  67.5 us
    pallas_call x1, Pallas kernels, project(): pl.pallas_call(functools.partial(project_kernel, prefix), out_shape=(jax....  47.3 us

profile of v2, /device:TPU:0, one launch (start us, length us, event | category | flops | bytes accessed | tf_op | source)
XLA Modules:
  0.0 116.5 jit_solution(7649068077546717406)
XLA Ops:
  0.0 47.3 %project.1 = (bf16[2,512,128]{2,1,0:T(8,128)(2,1)}, bf16[2,2,2304,128]{3,2,1,0:T(8,128)(2,1)}) custom-call(bf16[256,512]{1,0:T(8,128)(2,1)} %hid.1, f32[1,8192]{1,0:T(1,128)} %bitcast.5, f32[1,128]{1,0:T(1,128)} %constant.2.clone.freqs, bf16[8192,512]{1,0:T(8,128)(2,1)} %wq_hbm.1, bf16[64,8192]{1,0:T(8,128)(2,1)} %bitcast.3, bf16[64,8192]{1,0:T(8,128)(2,1)} %bitcast.4, ...), custom_call_target="tpu_custom_call" | custom-call | tf_op jit(solution)/shard_map/project/pallas_call | solution.py:266
  47.3 67.5 %attend_mix.1 = bf16[256,512]{1,0:T(8,128)(2,1)} custom-call(bf16[2,512,128]{2,1,0:T(8,128)(2,1)} %get-tuple-element.7.q, bf16[2,2,2304,128]{3,2,1,0:T(8,128)(2,1)} %get-tuple-element.8.kv, bf16[512,8192]{1,0:T(8,128)(2,1)} %w_hbm.1), custom_call_target="tpu_custom_call" | custom-call | tf_op jit(solution)/shard_map/attend_mix/pallas_call | solution.py:578
  114.8 1.7 %copy.10 = bf16[256,512]{1,0:T(8,128)(2,1)} copy(bf16[256,512]{1,0:T(8,128)(2,1)} %attend_mix.1) | data formatting | bytes 524288

commit v3 on v2

--- a/solution.py
+++ b/solution.py
@@ -15,7 +15,8 @@
 F32 = jnp.float32
 ROWS = 256
 FEATURES = 8192
-CHUNK = 256
+CUTS = ((0, 384), (384, 128))
+PIECES = ((0, 0, 1024), (0, 1024, 1024), (1, 0, 1024), (1, 1024, 1024), (0, 2048, 256), (1, 2048, 256))
 NEG = -1e30
 VMEM = pltpu.MemorySpace.VMEM
 
@@ -43,12 +44,19 @@
     )
 
 
-def project_kernel(
-    prefix, hid, gain, freqs, wq_hbm, wk_hbm, wv_hbm, cache,
-    q_out, kv_out,
-    got, wq, wkv, acc, squares, cos, sin, part, partner_part, fresh,
-    send, recv, load, swap_send, swap_recv,
+def block_kernel(
+    prefix, parts, hid, gain, freqs, wq_hbm, wk_hbm, wv_hbm, cache, w_hbm,
+    out,
+    got_a, got_b, w, wkv, acc, squares, cos, sin, part, partner_part, fresh, kv, vx,
+    qs, ob, oin, stat, stat_in, sa, sb, top_a, top_b, summed, att,
+    terms, relay, inbox, terms2, relay2, inbox2,
+    send, recv, load, w_load, swap_send, swap_recv,
+    q_send, q_recv, o_send, o_recv, t_send, t_recv, r_send, r_recv,
 ):
+    got = (got_a, got_b)
+    tokens = ROWS // parts
+    rows = 4 * tokens
+    half_rows = tokens // 2
     x, core, z, y = place()
     grp = 2 * x + core
     parity = lax.rem(y, 2)
@@ -59,8 +67,11 @@
     def to(dz, dy):
         return {"grp": grp, "tp": at(dz, dy)}
 
+    def chip(i):
+        return {"grp": 2 * wrap(i) + core, "tp": z * 4 + y}
+
     def chunk(half, a, b):
-        return 2 * (at(b, a) if half == 0 else at(a, b)) + half
+        return at(b, a) if half == 0 else at(a, b)
 
     def first(half, d):
         return to(0, d) if half == 0 else to(d, 0)
@@ -71,22 +82,23 @@
     partner = {"grp": grp, "tp": z * 4 + y + 1 - 2 * parity}
     sibling = {"grp": grp + 1 - 2 * core, "tp": z * 4 + y}
     loads = [
-        pltpu.make_async_copy(wq_hbm, wq, load.at[0]),
+        pltpu.make_async_copy(wq_hbm, w, load.at[0]),
         pltpu.make_async_copy(wk_hbm, wkv.at[pl.ds(0, 64)], load.at[1]),
         pltpu.make_async_copy(wv_hbm, wkv.at[pl.ds(64, 64)], load.at[2]),
     ]
     for one in loads:
         one.start()
-    own_cache = pltpu.make_async_copy(cache, kv_out.at[parity, core, pl.ds(0, 2048)], load.at[3])
+    own_cache = pltpu.make_async_copy(cache, kv.at[parity, core, pl.ds(0, 2048)], load.at[3])
     own_cache.start()
-    for half in range(2):
-        got[chunk(half, 0, 0)] = hid[:, half * CHUNK : (half + 1) * CHUNK]
-    greet([to(0, 1), to(0, -1), to(1, 0), to(-1, 0), sibling])
+    for half, (start, size) in enumerate(CUTS):
+        got[half][at(0, 0)] = hid[:, start : start + size]
+    order = (1, 3, 2)
+    greet([to(0, 1), to(0, -1), to(1, 0), to(-1, 0), sibling, chip(x + 1), chip(x + 2), chip(x + 3)])
 
     TOP, BOTTOM, ALL = pl.ds(0, 128), pl.ds(128, 128), pl.ds(0, 256)
 
     def message(half, m, idx, rows, partner):
-        ref = got.at[idx, rows]
+        ref = got[half].at[idx, rows]
         return remote(ref, ref, send.at[half, m], recv.at[half, m], partner)
 
     for m, d in ((0, 1), (1, -1)):
@@ -95,40 +107,32 @@
     for m, d in ((4, 1), (5, -1)):
         for half in range(2):
             message(half, m, chunk(half, 0, 0), ALL, second(half, d)).start()
-    mine = kv_out.at[parity, core, pl.ds(0, 2048)]
-    swaps = [
-        remote(cache, mine, swap_send.at[0], swap_recv.at[0], partner),
-        remote(cache, mine, swap_send.at[1], swap_recv.at[1], sibling),
-    ]
-    for one in swaps:
-        one.start()
-
     acc[...] = jnp.zeros_like(acc)
+    vx[:, :, 128:] = jnp.ones((2, 2304, 128), BF)
     squares[...] = jnp.zeros_like(squares)
 
-    def absorb(idx):
-        h = got[idx].astype(F32)
+    def absorb(half, t):
+        offset, size = CUTS[half]
+        h = got[half][t].astype(F32)
         sq = h * h
-        squares[...] += sq[:, :128] + sq[:, 128:]
-        depth = pl.ds(pl.multiple_of(idx * CHUNK, CHUNK), CHUNK)
+        sums = sq[:, :128]
+        for k in range(1, size // 128):
+            sums = sums + sq[:, k * 128 : (k + 1) * 128]
+        squares[...] += sums
+        depth = pl.ds(pl.multiple_of(t * 512 + offset, 128), size)
         scaled = (h * gain[:, depth]).astype(BF)
-        acc[:, :512] += jnp.dot(scaled, wq[depth, :], preferred_element_type=F32)
+        acc[:, :512] += jnp.dot(scaled, w[depth, :], preferred_element_type=F32)
         acc[:, 512:] += lax.dot_general(
             scaled, wkv[:, depth], (((1,), (1,)), ((), ())), preferred_element_type=F32
         )
 
-    def absorb_all(count, index_of):
+    def absorb_all(count, place_of):
         def step(i, carry):
-            absorb(index_of(i))
+            for half in range(2):
+                absorb(half, chunk(half, *place_of(i)))
             return carry
 
         lax.fori_loop(0, count, step, 0)
-
-    def pick(flag, a, b):
-        return jnp.where(flag == 0, a, b)
-
-    def chunk_of(half, a, b):
-        return pick(half, chunk(0, a, b), chunk(1, a, b))
 
     def arrived(half, m, idx, rows):
         message(half, m, idx, rows, sibling).wait_recv()
@@ -145,7 +149,7 @@
     sin[...] = jnp.where(lane < 64, -sine, sine)
     for one in loads:
         one.wait()
-    absorb_all(2, lambda i: chunk_of(i, 0, 0))
+    absorb_all(1, lambda i: (0, 0))
     for half in range(2):
         idx = chunk(half, -1, 0)
         arrived(half, 0, idx, ALL)
@@ -156,7 +160,14 @@
         arrived(half, 1, idx, ALL)
         message(half, 3, idx, BOTTOM, first(half, -1)).start()
         spread(half, 2, idx)
-    absorb_all(4, lambda i: chunk_of(i % 2, 2 * (i // 2) - 1, 0))
+    mine = kv.at[parity, core, pl.ds(0, 2048)]
+    swaps = [
+        remote(cache, mine, swap_send.at[0], swap_recv.at[0], partner),
+        remote(cache, mine, swap_send.at[1], swap_recv.at[1], sibling),
+    ]
+    for one in swaps:
+        one.start()
+    absorb_all(2, lambda i: (2 * i - 1, 0))
 
     def neighbours(j, a):
         for half in range(2):
@@ -166,14 +177,14 @@
             idx = chunk(half, a, 1)
             arrived(half, 5 + 4 * j, idx, ALL)
             message(half, 7 + 4 * j, idx, BOTTOM, second(half, -1)).start()
-        absorb_all(4, lambda i: chunk_of(i % 2, a, 2 * (i // 2) - 1))
+        absorb_all(2, lambda i: (a, 2 * i - 1))
 
     def opposite(j, a):
         for half in range(2):
             idx = chunk(half, a, 2)
             arrived(half, 6 + 4 * j, idx, TOP)
             arrived(half, 7 + 4 * j, idx, BOTTOM)
-        absorb_all(2, lambda i: chunk_of(i, a, 2))
+        absorb_all(1, lambda i: (a, 2))
 
     neighbours(0, 0)
     for half in range(2):
@@ -181,14 +192,14 @@
         arrived(half, 2, idx, TOP)
         arrived(half, 3, idx, BOTTOM)
         spread(half, 3, idx)
-    absorb_all(2, lambda i: chunk_of(i, 2, 0))
+    absorb_all(1, lambda i: (2, 0))
 
     def sweep(j, carry):
         neighbours(j, jnp.where(j == 1, -1, j - 1))
         return carry
 
     lax.fori_loop(1, 4, sweep, 0)
-    theirs = kv_out.at[1 - parity, core, pl.ds(0, 2048)]
+    theirs = kv.at[1 - parity, core, pl.ds(0, 2048)]
     remote(cache, theirs, swap_send.at[0], swap_recv.at[0], partner).wait_recv()
     passed = remote(theirs, theirs, swap_send.at[2], swap_recv.at[2], sibling)
     passed.start()
@@ -205,18 +216,31 @@
     part[...] = own.astype(BF)
     swap = remote(part, partner_part, swap_send.at[3], swap_recv.at[3], partner)
     swap.start()
-    c, s = cos[...], sin[...]
-
     def rope(v):
-        return v * c + pltpu.roll(v, 64, 1) * s
+        return v * cos[...] + pltpu.roll(v, 64, 1) * sin[...]
 
     scale = math.log2(math.e) / math.sqrt(HEAD_DIM)
-    parts = q_out.shape[0]
-    tokens = ROWS // parts
     for head in range(4):
         turned = (rope(acc[:, head * 128 : (head + 1) * 128] * root) * scale).astype(BF)
         for i in range(parts):
-            q_out[i, head * tokens : (head + 1) * tokens, :] = turned[i * tokens : (i + 1) * tokens, :]
+            qs[0, i, head * tokens : (head + 1) * tokens, :] = turned[i * tokens : (i + 1) * tokens, :]
+
+    def query(c, d):
+        return remote(qs.at[0, c], qs.at[d, c], q_send.at[d, c], q_recv.at[d, c], chip(x + d))
+
+    for c in range(parts):
+        for d in order:
+            query(c, d).start()
+
+    def fetch(t):
+        spot = w.at[pl.ds(pl.multiple_of(t * 512, 512), 512)]
+        return pltpu.make_async_copy(w_hbm.at[:, pl.ds(pl.multiple_of(t * 512, 512), 512)], spot, w_load.at[t])
+
+    def begin(t, carry):
+        fetch(t).start()
+        return carry
+
+    lax.fori_loop(0, 16, begin, 0)
     swap.wait()
     other = partner_part[...].astype(F32)
     left = jnp.where(parity == 0, own, other)
@@ -225,120 +249,18 @@
     value = jnp.where(lane < 64, pltpu.roll(left, 64, 1), right)
     fresh[0] = rope(key).astype(BF)
     fresh[1] = value.astype(BF)
-    spot = kv_out.at[:, core, pl.ds(2048, 256)]
+    spot = kv.at[:, core, pl.ds(2048, 256)]
     keep = pltpu.make_async_copy(fresh, spot, load.at[0])
     keep.start()
     give = remote(fresh, spot, swap_send.at[4], swap_recv.at[4], sibling)
     give.start()
-    keep.wait()
-    give.wait_send()
-    remote(fresh, kv_out.at[:, 1 - core, pl.ds(2048, 256)], swap_send.at[4], swap_recv.at[4], sibling).wait_recv()
     own_cache.wait()
-    swaps[0].wait_send()
-    swaps[1].wait_send()
-    remote(cache, kv_out.at[parity, 1 - core, pl.ds(0, 2048)], swap_send.at[1], swap_recv.at[1], sibling).wait_recv()
-    passed.wait_send()
+    remote(cache, kv.at[parity, 1 - core, pl.ds(0, 2048)], swap_send.at[1], swap_recv.at[1], sibling).wait_recv()
     remote(
-        cache, kv_out.at[1 - parity, 1 - core, pl.ds(0, 2048)], swap_send.at[2], swap_recv.at[2], sibling
+        cache, kv.at[1 - parity, 1 - core, pl.ds(0, 2048)], swap_send.at[2], swap_recv.at[2], sibling
     ).wait_recv()
-
-    def drain(half, m, rows):
-        message(half, m, chunk(half, 0, 0), rows, sibling).wait_send()
-
-    for half in range(2):
-        drain(half, 0, ALL)
-        drain(half, 1, ALL)
-        drain(half, 2, TOP)
-        drain(half, 3, BOTTOM)
-        for j in range(4):
-            drain(half, 4 + 4 * j, ALL)
-            drain(half, 5 + 4 * j, ALL)
-            drain(half, 6 + 4 * j, TOP)
-            drain(half, 7 + 4 * j, BOTTOM)
-
-
-def project(hid, gain, wq, wk, wv, cache, prefix, parts):
-    whole = pl.BlockSpec(memory_space=VMEM)
-    left = pl.BlockSpec(memory_space=pl.ANY)
-    dma = pltpu.SemaphoreType.DMA
-    half = np.arange(HEAD_DIM // 2, dtype=np.float64) * 2.0 / HEAD_DIM
-    freqs = jnp.asarray(np.tile(500000.0**-half, 2)[None, :], F32)
-    return pl.pallas_call(
-        functools.partial(project_kernel, prefix),
-        out_shape=(
-            jax.ShapeDtypeStruct((parts, 1024 // parts, 128), BF),
-            jax.ShapeDtypeStruct((2, 2, 2304, 128), BF),
-        ),
-        in_specs=[whole] * 3 + [left] * 4,
-        out_specs=(whole, left),
-        scratch_shapes=[
-            pltpu.VMEM((32, ROWS, CHUNK), BF),
-            pltpu.VMEM((FEATURES, 512), BF),
-            pltpu.VMEM((128, FEATURES), BF),
-            pltpu.VMEM((ROWS, 640), F32),
-            pltpu.VMEM((ROWS, 128), F32),
-            pltpu.VMEM((ROWS, 128), F32),
-            pltpu.VMEM((ROWS, 128), F32),
-            pltpu.VMEM((ROWS, 128), BF),
-            pltpu.VMEM((ROWS, 128), BF),
-            pltpu.VMEM((2, ROWS, 128), BF),
-            dma((2, 20)),
-            dma((2, 20)),
-            dma((4,)),
-            dma((5,)),
-            dma((5,)),
-        ],
-        compiler_params=pltpu.CompilerParams(
-            collective_id=0, has_side_effects=True, vmem_limit_bytes=60 << 20
-        ),
-        name="project",
-    )(hid, gain, freqs, wq, wk.T, wv.T, cache)
-
-
-PIECES = ((0, 1024), (1024, 1024), (2048, 256))
-
-
-def attend_mix_kernel(
-    q, kv, w_hbm, out,
-    w, vx, qs, ob, oin, stat, stat_in, sa, sb, top_a, top_b, summed, att,
-    terms, relay, inbox, terms2, relay2, inbox2,
-    q_send, q_recv, o_send, o_recv, t_send, t_recv, send, recv, load,
-):
-    x, core, z, y = place()
-    grp = 2 * x + core
-    tp = z * 4 + y
-    parts, rows, width = q.shape
-    tokens = rows // 4
-    half_rows = tokens // 2
-
-    def chip(i):
-        return {"grp": 2 * wrap(i) + core, "tp": tp}
-
-    def to(dz, dy):
-        return {"grp": grp, "tp": wrap(z + dz) * 4 + wrap(y + dy)}
-
-    def first(half, d):
-        return to(0, d) if half == 0 else to(d, 0)
-
-    def second(half, d):
-        return to(d, 0) if half == 0 else to(0, d)
-
+    vx[:, :2048, :128] = kv[1, :, :2048]
     here = ((y, z), (z, y))
-    fetch = pltpu.make_async_copy(w_hbm, w, load.at[0])
-    fetch.start()
-    greet([chip(x + 1), chip(x + 2), chip(x + 3), to(0, 1), to(0, -1), to(1, 0), to(-1, 0)])
-    order = (1, 3, 2)
-
-    def query(c, d):
-        return remote(q.at[c], qs.at[d, c], q_send.at[d, c], q_recv.at[d, c], chip(x + d))
-
-    for c in range(parts):
-        for d in order:
-            query(c, d).start()
-    qs[0] = q[...]
-    for b in range(2):
-        vx[b, :, :128] = kv[1, b]
-        vx[b, :, 128:] = jnp.ones((2304, 128), BF)
     diff = lax.broadcasted_iota(jnp.int32, (rows, 256), 1) - lax.rem(
         lax.broadcasted_iota(jnp.int32, (rows, 256), 0), tokens
     )
@@ -353,11 +275,11 @@
 
         @pl.when(slot != 0)
         def _():
-            remote(q.at[0], qs.at[slot, c], q_send.at[slot, c], q_recv.at[slot, c], chip(x + 1)).wait_recv()
+            remote(qs.at[0, 0], qs.at[slot, c], q_send.at[slot, c], q_recv.at[slot, c], chip(x + 1)).wait_recv()
 
     def score(i, n, s_ref, top_ref):
         c, slot = block_of(i)
-        b, (start, size) = n // 3, PIECES[n % 3]
+        b, start, size = PIECES[n]
         s = lax.dot_general(
             qs[slot, c], kv[0, b, start : start + size, :], (((1,), (1,)), ((), ())), preferred_element_type=F32
         )
@@ -371,17 +293,17 @@
         top_ref[...] = top if n == 0 else jnp.maximum(top_ref[...], top)
 
     def weigh(n, s_ref, best):
-        b, (start, size) = n // 3, PIECES[n % 3]
-        w_ = jnp.exp2(s_ref[:, b * 2304 + start : b * 2304 + start + size] - best)
-        o = jnp.dot(w_.astype(BF), vx[b, start : start + size, :], preferred_element_type=F32)
+        b, start, size = PIECES[n]
+        p = jnp.exp2(s_ref[:, b * 2304 + start : b * 2304 + start + size] - best)
+        o = jnp.dot(p.astype(BF), vx[b, start : start + size, :], preferred_element_type=F32)
         summed[...] = o if n == 0 else summed[...] + o
 
-    lane = lax.broadcasted_iota(jnp.int32, (rows, 128), 1)
+    wide = lax.broadcasted_iota(jnp.int32, (rows, 128), 1)
 
     def settle(i, best):
         c, slot = block_of(i)
         ob[slot, c] = summed[:, :128].astype(BF)
-        both = jnp.where(lane == 0, best, summed[:, 128:])
+        both = jnp.where(wide == 0, best, summed[:, 128:])
         stat[slot, c] = both.T[:8, :]
 
         @pl.when(slot != 0)
@@ -417,8 +339,8 @@
 
         def step(b, carry):
             t = b * 4 + a if half == 0 else a * 4 + b
-            start = pl.multiple_of(t * 512 + half * 256, 256)
-            r = jnp.dot(att[...], w[:, pl.ds(start, 256)], preferred_element_type=F32).astype(BF)
+            deep = pl.ds(pl.multiple_of(t * 512, 512), 512)
+            r = jnp.dot(att[...], w[deep, half * 256 : (half + 1) * 256], preferred_element_type=F32).astype(BF)
             terms[c, half, a, 0, b] = r[:half_rows]
             terms[c, half, a, 1, b] = r[half_rows:]
             return carry
@@ -426,7 +348,7 @@
         lax.fori_loop(0, 4, step, 0)
 
     def copy(c, half, m, src, dst, partner):
-        return remote(src, dst, send.at[c, half, m], recv.at[c, half, m], partner)
+        return remote(src, dst, r_send.at[c, half, m], r_recv.at[c, half, m], partner)
 
     def moves(c, half):
         def block(d, ch):
@@ -516,7 +438,12 @@
 
     blocks = 4 * parts
     prepare(0)
-    for n in range(6):
+    for n in range(4):
+        score(0, n, sa, top_a)
+    keep.wait()
+    remote(fresh, kv.at[:, 1 - core, pl.ds(2048, 256)], swap_send.at[4], swap_recv.at[4], sibling).wait_recv()
+    vx[:, 2048:, :128] = kv[1, :, 2048:]
+    for n in range(4, 6):
         score(0, n, sa, top_a)
 
     def half_step(i, now, top_now, later, top_later):
@@ -532,33 +459,38 @@
             weigh(n, now, best)
         settle(i, best)
 
+    def fetched(t, carry):
+        fetch(t).wait()
+        return carry
+
     def step(p, carry):
+        half_step(2 * p, sa, top_a, sb, top_b)
+
+        @pl.when(p == 2)
+        def _():
+            lax.fori_loop(0, 16, fetched, 0)
+            stage0(0)
+
         @pl.when(p == 3)
         def _():
             stage1(0)
 
-        half_step(2 * p, sa, top_a, sb, top_b)
-
-        @pl.when(p == 2)
-        def _():
-            fetch.wait()
-            stage0(0)
-
-        @pl.when(p == 3)
-        def _():
-            stage2(0)
-
         half_step(2 * p + 1, sb, top_b, sa, top_a)
         return carry
 
     lax.fori_loop(0, blocks // 2, step, 0)
+    stage2(0)
+    stage0(1)
     stage3(0)
-    stage0(1)
+    stage1(1)
     stage4(0)
-    stage1(1)
     stage2(1)
     stage3(1)
     stage4(1)
+    give.wait_send()
+    swaps[0].wait_send()
+    swaps[1].wait_send()
+    passed.wait_send()
     for c in range(parts):
         for d in order:
             query(c, d).wait_send()
@@ -569,19 +501,47 @@
             for m in range(12):
                 sends(m).wait_send()
 
-
-def attend_mix(q, kv, w_out):
-    parts, rows, width = q.shape
+    def drain(half, m, rows):
+        message(half, m, chunk(half, 0, 0), rows, sibling).wait_send()
+
+    for half in range(2):
+        drain(half, 0, ALL)
+        drain(half, 1, ALL)
+        drain(half, 2, TOP)
+        drain(half, 3, BOTTOM)
+        for j in range(4):
+            drain(half, 4 + 4 * j, ALL)
+            drain(half, 5 + 4 * j, ALL)
+            drain(half, 6 + 4 * j, TOP)
+            drain(half, 7 + 4 * j, BOTTOM)
+
+
+def block(hid, gain, wq, wk, wv, cache, w_out, prefix, parts):
     whole = pl.BlockSpec(memory_space=VMEM)
+    left = pl.BlockSpec(memory_space=pl.ANY)
     dma = pltpu.SemaphoreType.DMA
+    half = np.arange(HEAD_DIM // 2, dtype=np.float64) * 2.0 / HEAD_DIM
+    freqs = jnp.asarray(np.tile(500000.0**-half, 2)[None, :], F32)
+    rows = 4 * ROWS // parts
     h = rows // 8
     return pl.pallas_call(
-        attend_mix_kernel,
+        functools.partial(block_kernel, prefix, parts),
         out_shape=jax.ShapeDtypeStruct((ROWS, 512), BF),
-        in_specs=[whole, whole, pl.BlockSpec(memory_space=pl.ANY)],
+        in_specs=[whole] * 3 + [left] * 5,
         out_specs=whole,
         scratch_shapes=[
-            pltpu.VMEM((512, FEATURES), BF),
+            pltpu.VMEM((16, ROWS, CUTS[0][1]), BF),
+            pltpu.VMEM((16, ROWS, CUTS[1][1]), BF),
+            pltpu.VMEM((FEATURES, 512), BF),
+            pltpu.VMEM((128, FEATURES), BF),
+            pltpu.VMEM((ROWS, 640), F32),
+            pltpu.VMEM((ROWS, 128), F32),
+            pltpu.VMEM((ROWS, 128), F32),
+            pltpu.VMEM((ROWS, 128), F32),
+            pltpu.VMEM((ROWS, 128), BF),
+            pltpu.VMEM((ROWS, 128), BF),
+            pltpu.VMEM((2, ROWS, 128), BF),
+            pltpu.VMEM((2, 2, 2304, 128), BF),
             pltpu.VMEM((2, 2304, 256), BF),
             pltpu.VMEM((4, parts, rows, 128), BF),
             pltpu.VMEM((4, parts, rows, 128), BF),
@@ -600,20 +560,25 @@
             pltpu.VMEM((parts, 2, 2, 4, h, 256), BF),
             pltpu.VMEM((parts, 2, 2, h, 256), BF),
             pltpu.VMEM((parts, 2, 2, 2, h, 256), BF),
+            dma((2, 20)),
+            dma((2, 20)),
+            dma((4,)),
+            dma((16,)),
+            dma((5,)),
+            dma((5,)),
         ]
         + [dma((4, parts))] * 6
-        + [dma((parts, 2, 12)), dma((parts, 2, 12)), dma((1,))],
+        + [dma((parts, 2, 12)), dma((parts, 2, 12))],
         compiler_params=pltpu.CompilerParams(
-            collective_id=1, has_side_effects=True, vmem_limit_bytes=60 << 20
+            collective_id=0, has_side_effects=True, vmem_limit_bytes=62 << 20
         ),
-        name="attend_mix",
-    )(q, kv, w_out)
+        name="block",
+    )(hid, gain, freqs, wq, wk.T, wv.T, cache, w_out)
 
 
 def body(prefix, parts, hidden_states, norm_gain, w_query, w_key, w_value, cache, w_out):
     gain = norm_gain.reshape(1, FEATURES)
-    q, kv = project(hidden_states, gain, w_query, w_key, w_value, cache, prefix, parts)
-    return attend_mix(q, kv, w_out)
+    return block(hidden_states, gain, w_query, w_key, w_value, cache, w_out, prefix, parts)
 
 
 def solution(mesh):

time: 117 us -> 103 us (0.88)
  Pallas kernels: 115 us -> 101 us
    pallas_call x2 -> x1, Pallas kernels: 115 us -> 101 us  [block(): pl.pallas_call(functools.partial(block_kernel, prefix, parts), out_shape=...]
where the time goes in v3:
time: 103 us
  Pallas kernels  101 us (98%)
  local copies, waits for them, and re-layouts  1.67 us (2%)
    pallas_call x1, Pallas kernels, block(): pl.pallas_call(functools.partial(block_kernel, prefix, parts), out_shape=...  101 us

profile of v3, /device:TPU:0, one launch (start us, length us, event | category | flops | bytes accessed | tf_op | source)
XLA Modules:
  0.0 102.5 jit_solution(15089216569951837565)
XLA Ops:
  0.0 100.8 %block.1 = bf16[256,512]{1,0:T(8,128)(2,1)} custom-call(bf16[256,512]{1,0:T(8,128)(2,1)} %hid.1, f32[1,8192]{1,0:T(1,128)} %bitcast.5, f32[1,128]{1,0:T(1,128)} %constant.2.clone.freqs, bf16[8192,512]{1,0:T(8,128)(2,1)} %wq_hbm.1, bf16[64,8192]{1,0:T(8,128)(2,1)} %bitcast.3, bf16[64,8192]{1,0:T(8,128)(2,1)} %bitcast.4, bf16[2048,128]{1,0:T(8,128)(2,1)} %cache.1, ...), custom_call_target="tpu_custom_call" | custom-call | tf_op jit(solution)/shard_map/block/pallas_call | solution.py:527
  100.8 1.7 %copy.10 = bf16[256,512]{1,0:T(8,128)(2,1)} copy(bf16[256,512]{1,0:T(8,128)(2,1)} %block.1) | data formatting | bytes 524288

commit v4 on v3

--- a/solution.py
+++ b/solution.py
@@ -15,7 +15,7 @@
 F32 = jnp.float32
 ROWS = 256
 FEATURES = 8192
-CUTS = ((0, 384), (384, 128))
+CUTS = ((0, 160), (160, 96))
 PIECES = ((0, 0, 1024), (0, 1024, 1024), (1, 0, 1024), (1, 1024, 1024), (0, 2048, 256), (1, 2048, 256))
 NEG = -1e30
 VMEM = pltpu.MemorySpace.VMEM
@@ -91,14 +91,17 @@
     own_cache = pltpu.make_async_copy(cache, kv.at[parity, core, pl.ds(0, 2048)], load.at[3])
     own_cache.start()
     for half, (start, size) in enumerate(CUTS):
-        got[half][at(0, 0)] = hid[:, start : start + size]
+        got[half][at(0, 0)] = hid[start : start + size, :]
     order = (1, 3, 2)
     greet([to(0, 1), to(0, -1), to(1, 0), to(-1, 0), sibling, chip(x + 1), chip(x + 2), chip(x + 3)])
 
-    TOP, BOTTOM, ALL = pl.ds(0, 128), pl.ds(128, 128), pl.ds(0, 256)
-
-    def message(half, m, idx, rows, partner):
-        ref = got[half].at[idx, rows]
+    TOP, BOTTOM, ALL = 0, 1, 2
+    on = jnp.where(parity == 0, -1, 1)
+    passes, takes = 3 - parity, 2 + parity
+
+    def message(half, m, idx, which, partner):
+        size = CUTS[half][1]
+        ref = got[half].at[idx, pl.ds(which % 2 * size // 2, size if which == ALL else size // 2)]
         return remote(ref, ref, send.at[half, m], recv.at[half, m], partner)
 
     for m, d in ((0, 1), (1, -1)):
@@ -112,17 +115,15 @@
     squares[...] = jnp.zeros_like(squares)
 
     def absorb(half, t):
-        offset, size = CUTS[half]
+        start, size = CUTS[half]
+        here = slice(start, start + size)
         h = got[half][t].astype(F32)
         sq = h * h
-        sums = sq[:, :128]
-        for k in range(1, size // 128):
-            sums = sums + sq[:, k * 128 : (k + 1) * 128]
-        squares[...] += sums
-        depth = pl.ds(pl.multiple_of(t * 512 + offset, 128), size)
+        squares[here] += sq[:, :128] + sq[:, 128:256] + sq[:, 256:384] + sq[:, 384:]
+        depth = pl.ds(pl.multiple_of(t * 512, 512), 512)
         scaled = (h * gain[:, depth]).astype(BF)
-        acc[:, :512] += jnp.dot(scaled, w[depth, :], preferred_element_type=F32)
-        acc[:, 512:] += lax.dot_general(
+        acc[here, :512] += jnp.dot(scaled, w[depth, :], preferred_element_type=F32)
+        acc[here, 512:] += lax.dot_general(
             scaled, wkv[:, depth], (((1,), (1,)), ((), ())), preferred_element_type=F32
         )
 
@@ -153,12 +154,16 @@
     for half in range(2):
         idx = chunk(half, -1, 0)
         arrived(half, 0, idx, ALL)
-        message(half, 2, idx, TOP, first(half, 1)).start()
+        if half == 1:
+            message(half, 2, idx, TOP, first(half, 1)).start()
         spread(half, 1, idx)
     for half in range(2):
         idx = chunk(half, 1, 0)
         arrived(half, 1, idx, ALL)
-        message(half, 3, idx, BOTTOM, first(half, -1)).start()
+        if half == 1:
+            message(half, 3, idx, BOTTOM, first(half, -1)).start()
+        else:
+            message(half, passes, chunk(half, -on, 0), ALL, first(half, on)).start()
         spread(half, 2, idx)
     mine = kv.at[parity, core, pl.ds(0, 2048)]
     swaps = [
@@ -173,24 +178,34 @@
         for half in range(2):
             idx = chunk(half, a, -1)
             arrived(half, 4 + 4 * j, idx, ALL)
-            message(half, 6 + 4 * j, idx, TOP, second(half, 1)).start()
+            if half == 0:
+                message(half, 6 + 4 * j, idx, TOP, second(half, 1)).start()
             idx = chunk(half, a, 1)
             arrived(half, 5 + 4 * j, idx, ALL)
-            message(half, 7 + 4 * j, idx, BOTTOM, second(half, -1)).start()
+            if half == 0:
+                message(half, 7 + 4 * j, idx, BOTTOM, second(half, -1)).start()
+            else:
+                message(half, 4 + passes + 4 * j, chunk(half, a, -on), ALL, second(half, on)).start()
         absorb_all(2, lambda i: (a, 2 * i - 1))
 
     def opposite(j, a):
         for half in range(2):
             idx = chunk(half, a, 2)
-            arrived(half, 6 + 4 * j, idx, TOP)
-            arrived(half, 7 + 4 * j, idx, BOTTOM)
+            if half == 0:
+                arrived(half, 6 + 4 * j, idx, TOP)
+                arrived(half, 7 + 4 * j, idx, BOTTOM)
+            else:
+                arrived(half, 4 + takes + 4 * j, idx, ALL)
         absorb_all(1, lambda i: (a, 2))
 
     neighbours(0, 0)
     for half in range(2):
         idx = chunk(half, 2, 0)
-        arrived(half, 2, idx, TOP)
-        arrived(half, 3, idx, BOTTOM)
+        if half == 1:
+            arrived(half, 2, idx, TOP)
+            arrived(half, 3, idx, BOTTOM)
+        else:
+            arrived(half, takes, idx, ALL)
         spread(half, 3, idx)
     absorb_all(1, lambda i: (2, 0))
 
@@ -345,7 +360,7 @@
             terms[c, half, a, 1, b] = r[half_rows:]
             return carry
 
-        lax.fori_loop(0, 4, step, 0)
+        lax.fori_loop(0, 4, step, 0, unroll=True)
 
     def copy(c, half, m, src, dst, partner):
         return remote(src, dst, r_send.at[c, half, m], r_recv.at[c, half, m], partner)
@@ -413,7 +428,7 @@
                     terms2[c, half, ch, b] = got.astype(BF)
                 return carry
 
-            lax.fori_loop(0, 4, merge, 0)
+            lax.fori_loop(0, 4, merge, 0, unroll=True)
             for m in (6, 7, 8, 10):
                 sends(m).start()
 
@@ -507,13 +522,19 @@
     for half in range(2):
         drain(half, 0, ALL)
         drain(half, 1, ALL)
-        drain(half, 2, TOP)
-        drain(half, 3, BOTTOM)
+        if half == 1:
+            drain(half, 2, TOP)
+            drain(half, 3, BOTTOM)
+        else:
+            drain(half, passes, ALL)
         for j in range(4):
             drain(half, 4 + 4 * j, ALL)
             drain(half, 5 + 4 * j, ALL)
-            drain(half, 6 + 4 * j, TOP)
-            drain(half, 7 + 4 * j, BOTTOM)
+            if half == 0:
+                drain(half, 6 + 4 * j, TOP)
+                drain(half, 7 + 4 * j, BOTTOM)
+            else:
+                drain(half, 4 + passes + 4 * j, ALL)
 
 
 def block(hid, gain, wq, wk, wv, cache, w_out, prefix, parts):
@@ -530,8 +551,8 @@
         in_specs=[whole] * 3 + [left] * 5,
         out_specs=whole,
         scratch_shapes=[
-            pltpu.VMEM((16, ROWS, CUTS[0][1]), BF),
-            pltpu.VMEM((16, ROWS, CUTS[1][1]), BF),
+            pltpu.VMEM((16, CUTS[0][1], 512), BF),
+            pltpu.VMEM((16, CUTS[1][1], 512), BF),
             pltpu.VMEM((FEATURES, 512), BF),
             pltpu.VMEM((128, FEATURES), BF),
             pltpu.VMEM((ROWS, 640), F32),

time: 103 us -> 97.8 us (0.950)
  Pallas kernels: 101 us -> 95.8 us
    pallas_call x1, Pallas kernels: 101 us -> 95.8 us  [block(): pl.pallas_call(functools.partial(block_kernel, prefix, parts), out_shape=...]
where the time goes in v4:
time: 97.8 us; the launch traced here: 97.5 us
  Pallas kernels  95.8 us (98%)
  local copies, waits for them, and re-layouts  1.67 us (2%)
    pallas_call x1, Pallas kernels, block(): pl.pallas_call(functools.partial(block_kernel, prefix, parts), out_shape=...  95.8 us

profile of v4, /device:TPU:0, one launch (start us, length us, event | category | flops | bytes accessed | tf_op | source)
XLA Modules:
  0.0 97.5 jit_solution(10996170229860244520)
XLA Ops:
  0.0 95.8 %block.1 = bf16[256,512]{1,0:T(8,128)(2,1)} custom-call(bf16[256,512]{1,0:T(8,128)(2,1)} %hid.1, f32[1,8192]{1,0:T(1,128)} %bitcast.5, f32[1,128]{1,0:T(1,128)} %constant.2.clone.freqs, bf16[8192,512]{1,0:T(8,128)(2,1)} %wq_hbm.1, bf16[64,8192]{1,0:T(8,128)(2,1)} %bitcast.3, bf16[64,8192]{1,0:T(8,128)(2,1)} %bitcast.4, bf16[2048,128]{1,0:T(8,128)(2,1)} %cache.1, ...), custom_call_target="tpu_custom_call" | custom-call | tf_op jit(solution)/shard_map/block/pallas_call | solution.py:548
  95.8 1.7 %copy.10 = bf16[256,512]{1,0:T(8,128)(2,1)} copy(bf16[256,512]{1,0:T(8,128)(2,1)} %block.1) | data formatting | bytes 524288

commit v5 on v4

--- a/solution.py
+++ b/solution.py
@@ -92,7 +92,7 @@
     own_cache.start()
     for half, (start, size) in enumerate(CUTS):
         got[half][at(0, 0)] = hid[start : start + size, :]
-    order = (1, 3, 2)
+    order = (3, 2, 1)
     greet([to(0, 1), to(0, -1), to(1, 0), to(-1, 0), sibling, chip(x + 1), chip(x + 2), chip(x + 3)])
 
     TOP, BOTTOM, ALL = 0, 1, 2
@@ -283,7 +283,7 @@
     def block_of(i):
         c, k = i // 4, lax.rem(i, 4)
         k = jnp.where(c == 0, k, lax.rem(k + 1, 4))
-        return c, jnp.where(k == 2, 3, jnp.where(k == 3, 2, k))
+        return c, jnp.where(k == 0, 0, 4 - k)
 
     def prepare(i):
         c, slot = block_of(i)

time: 97.8 us -> 97.2 us (level); the launches traced: 97.5 us -> 95.5 us
  Pallas kernels: 95.8 us -> 93.9 us
    pallas_call x1, Pallas kernels: 95.8 us -> 93.9 us  [block(): pl.pallas_call(functools.partial(block_kernel, prefix, parts), out_shape=...]
where the time goes in v5:
time: 97.2 us; the launch traced here: 95.5 us
  Pallas kernels  93.9 us (97%)
  local copies, waits for them, and re-layouts  1.67 us (2%)
    pallas_call x1, Pallas kernels, block(): pl.pallas_call(functools.partial(block_kernel, prefix, parts), out_shape=...  93.9 us

profile of v5, /device:TPU:0, one launch (start us, length us, event | category | flops | bytes accessed | tf_op | source)
XLA Modules:
  0.0 95.5 jit_solution(2033240147342852949)
XLA Ops:
  0.0 93.9 %block.1 = bf16[256,512]{1,0:T(8,128)(2,1)} custom-call(bf16[256,512]{1,0:T(8,128)(2,1)} %hid.1, f32[1,8192]{1,0:T(1,128)} %bitcast.5, f32[1,128]{1,0:T(1,128)} %constant.2.clone.freqs, bf16[8192,512]{1,0:T(8,128)(2,1)} %wq_hbm.1, bf16[64,8192]{1,0:T(8,128)(2,1)} %bitcast.3, bf16[64,8192]{1,0:T(8,128)(2,1)} %bitcast.4, bf16[2048,128]{1,0:T(8,128)(2,1)} %cache.1, ...), custom_call_target="tpu_custom_call" | custom-call | tf_op jit(solution)/shard_map/block/pallas_call | solution.py:548
  93.9 1.7 %copy.10 = bf16[256,512]{1,0:T(8,128)(2,1)} copy(bf16[256,512]{1,0:T(8,128)(2,1)} %block.1) | data formatting | bytes 524288

commit v6 on v5

--- a/solution.py
+++ b/solution.py
@@ -110,6 +110,13 @@
     for m, d in ((4, 1), (5, -1)):
         for half in range(2):
             message(half, m, chunk(half, 0, 0), ALL, second(half, d)).start()
+    mine = kv.at[parity, core, pl.ds(0, 2048)]
+    swaps = [
+        remote(cache, mine, swap_send.at[0], swap_recv.at[0], partner),
+        remote(cache, mine, swap_send.at[1], swap_recv.at[1], sibling),
+    ]
+    for one in swaps:
+        one.start()
     acc[...] = jnp.zeros_like(acc)
     vx[:, :, 128:] = jnp.ones((2, 2304, 128), BF)
     squares[...] = jnp.zeros_like(squares)
@@ -165,13 +172,6 @@
         else:
             message(half, passes, chunk(half, -on, 0), ALL, first(half, on)).start()
         spread(half, 2, idx)
-    mine = kv.at[parity, core, pl.ds(0, 2048)]
-    swaps = [
-        remote(cache, mine, swap_send.at[0], swap_recv.at[0], partner),
-        remote(cache, mine, swap_send.at[1], swap_recv.at[1], sibling),
-    ]
-    for one in swaps:
-        one.start()
     absorb_all(2, lambda i: (2 * i - 1, 0))
 
     def neighbours(j, a):

time: 97.2 us -> 97.3 us (level)
  no operation moved by 1% of the time
where the time goes in v6:
time: 97.3 us; the launch traced here: 96 us
  Pallas kernels  94.3 us (97%)
  local copies, waits for them, and re-layouts  1.67 us (2%)
    pallas_call x1, Pallas kernels, block(): pl.pallas_call(functools.partial(block_kernel, prefix, parts), out_shape=...  94.3 us

profile of v6, /device:TPU:0, one launch (start us, length us, event | category | flops | bytes accessed | tf_op | source)
XLA Modules:
  0.0 96.0 jit_solution(14424714664215148734)
XLA Ops:
  0.0 94.3 %block.1 = bf16[256,512]{1,0:T(8,128)(2,1)} custom-call(bf16[256,512]{1,0:T(8,128)(2,1)} %hid.1, f32[1,8192]{1,0:T(1,128)} %bitcast.5, f32[1,128]{1,0:T(1,128)} %constant.2.clone.freqs, bf16[8192,512]{1,0:T(8,128)(2,1)} %wq_hbm.1, bf16[64,8192]{1,0:T(8,128)(2,1)} %bitcast.3, bf16[64,8192]{1,0:T(8,128)(2,1)} %bitcast.4, bf16[2048,128]{1,0:T(8,128)(2,1)} %cache.1, ...), custom_call_target="tpu_custom_call" | custom-call | tf_op jit(solution)/shard_map/block/pallas_call | solution.py:548
  94.3 1.7 %copy.10 = bf16[256,512]{1,0:T(8,128)(2,1)} copy(bf16[256,512]{1,0:T(8,128)(2,1)} %block.1) | data formatting | bytes 524288
